TPU v7x, 32 devices: a whole 2x2x4 slice. The times are simulated.
32 devices in a mesh: grp: 2 (over y), seq: 4 (over z), tp: 4 (over x, core).
Axes of the slice: x: 2, y: 2, z: 4, core: 2. Of those that a mesh axis runs over, the one named last changes fastest.
Arguments:
- ssm_input: bfloat16 [2048, 8192], P(('grp', 'seq'), 'tp'), parts along dimension 0, may hold values from -6 to 6
- bmat: bfloat16 [2048, 1024], P(('grp', 'seq'), 'tp'), parts along dimension 0, may hold values from -6 to 6
- cmat: bfloat16 [2048, 1024], P(('grp', 'seq'), 'tp'), parts along dimension 0, may hold values from -6 to 6
- dt_raw: bfloat16 [2048, 128], P(('grp', 'seq'), 'tp'), parts along dimension 0
- a_log: float32 [128], P('tp'), may hold values from -0.5 to 0.5
- d_skip: float32 [128], P('tp'), may hold values from 0.5 to 1.5
- prompt_len: int32 [16], P('grp'), parts along dimension 0, may hold values from 1 to 1024, as said below
- owner: int32 [16], P('grp'), parts along dimension 0, may hold values from 0 to 3, as said below
- dec_x: bfloat16 [8, 4, 4, 8192], P(('grp', 'seq'), None, None, 'tp'), parts along dimension 0, may hold values from -6 to 6
- dec_b: bfloat16 [8, 4, 4, 1024], P(('grp', 'seq'), None, None, 'tp'), parts along dimension 0, may hold values from -6 to 6
- dec_c: bfloat16 [8, 4, 4, 1024], P(('grp', 'seq'), None, None, 'tp'), parts along dimension 0, may hold values from -6 to 6
- dec_dt: bfloat16 [8, 4, 4, 128], P(('grp', 'seq'), None, None, 'tp'), parts along dimension 0
Outputs:
- prefill_out: bfloat16 [2048, 8192], P(('grp', 'seq'), 'tp'), parts along dimension 0
- decode_out: bfloat16 [8, 4, 4, 8192], P(('grp', 'seq'), None, None, 'tp'), parts along dimension 0
There are 2 independent parts, one for each index of `grp`. A program takes and returns all parts, laid end to end along the dimension named above; an argument that names none is the same for every part. Nothing has to cross between parts.
Inputs may be any that keep to these rules, and one draw needn't show every extreme that they name: `prompt_len`: no two requests have both the same owner and the same 256-position part of the prompt holding their last prompt position. Each owner decodes at most 4 requests and each part holds the last position of at most 4; some owner and some part reach that in every draw. `owner`: every index of seq owns at least one request.
All inputs are finite; a program needn't handle non-finite values.
Results may differ from a plain program's by a relative error of at most 0.0055.
Values may be sent and summed in bfloat16 or wider, within the bound.
A program may use at most 128 MiB of HBM per device.

v0:
```python
import math

import jax
import jax.numpy as jnp
from jax import lax
from jax.sharding import PartitionSpec as P

H = 128
P_SIZE = 64
N = 128
G = 8
SPAN = 128
STEPS = 4


def carried_in(value, axis, join, neutral):
    count, mine = (lax.axis_size(axis), lax.axis_index(axis))
    pieces = jax.tree.map(lambda part: lax.all_gather(part, axis), value)
    total = jax.tree.map(
        lambda part, zero: jnp.full_like(part, 0) + jnp.asarray(zero, part.dtype), value, neutral
    )

    def lap(position, total):
        longer = join(total, jax.tree.map(lambda part: part[position], pieces))
        return jax.tree.map(lambda new, old: jnp.where(position < mine, new, old), longer, total)

    return lax.fori_loop(0, count - 1, lap, total)


def blocked(function, arrays, batch_size):
    leading = arrays[0].shape[0]
    split = tuple(
        (item.reshape((leading // batch_size, batch_size) + item.shape[1:]) for item in arrays)
    )
    results = lax.map(lambda items: jax.vmap(function)(*items), split)
    return jax.tree.map(lambda value: value.reshape((leading,) + value.shape[2:]), results)


def shards(
    ssm_input, bmat, cmat, dt_raw, a_log, d_skip, prompt_len, owner, dec_x, dec_b, dec_c, dec_dt
):
    highest = lax.Precision.HIGHEST
    tensor_count = lax.axis_size("tp")
    seq_count = lax.axis_size("seq")
    my_index = lax.axis_index("seq")
    heads_here = H // tensor_count
    groups_here = G // tensor_count
    per_group = H // G
    token_count = ssm_input.shape[0]
    span_count = token_count // SPAN
    step_size = jax.nn.softplus(dt_raw.astype(jnp.float32))
    log_decay = -jnp.exp(a_log)[None, :] * step_size
    cumulative = jnp.cumsum(log_decay.reshape(span_count, SPAN, heads_here), axis=1)
    step_spans = step_size.reshape(span_count, SPAN, heads_here)
    x_spans = ssm_input.reshape(span_count, SPAN, heads_here, P_SIZE)
    b_spans = bmat.reshape(span_count, SPAN, groups_here, N)
    c_spans = cmat.reshape(span_count, SPAN, groups_here, N)
    causal = jnp.arange(SPAN)[:, None] >= jnp.arange(SPAN)[None, :]

    def group_scaled(b_part, factor):
        grouped = factor.reshape(SPAN, groups_here, per_group)[:, :, :, None]
        product = b_part.astype(jnp.float32)[:, :, None, :] * grouped
        return product.astype(jnp.bfloat16).reshape(SPAN, heads_here, N)

    def span_local(x_part, b_part, c_part, cum_part, step_part):
        score_values = jnp.einsum(
            "tgn,sgn->gts", c_part, b_part, preferred_element_type=jnp.float32
        )
        head_scores = jnp.repeat(score_values, per_group, axis=0)
        spread = cum_part.T[:, :, None] - cum_part.T[:, None, :]
        decay = jnp.where(causal[None], jnp.exp(jnp.where(causal[None], spread, 0.0)), 0.0)
        weights = (head_scores * decay * step_part.T[:, None, :]).astype(jnp.bfloat16)
        inner = jnp.einsum("hts,shp->thp", weights, x_part, preferred_element_type=jnp.float32)
        scaled = group_scaled(b_part, jnp.exp(cum_part[-1][None, :] - cum_part) * step_part)
        span_state = jnp.einsum("shp,shn->hpn", x_part, scaled, preferred_element_type=jnp.float32)
        return (inner, span_state)

    inner_all, span_states = blocked(
        span_local, (x_spans, b_spans, c_spans, cumulative, step_spans), math.gcd(4, span_count)
    )
    block_ends = cumulative[:, -1, :]

    def carry_local(state, items):
        ending, span_state = items
        return (jnp.exp(ending)[:, None, None] * state + span_state, state)

    zero_state = jnp.zeros((heads_here, P_SIZE, N), jnp.float32)
    local_total, local_starts = lax.scan(carry_local, zero_state, (block_ends, span_states))

    def combine(earlier, later):
        return (earlier[0] + later[0], jnp.exp(later[0])[:, None, None] * earlier[1] + later[1])

    device_decay = jnp.sum(block_ends, axis=0)
    incoming = carried_in(
        (device_decay, local_total),
        "seq",
        combine,
        (jnp.zeros((heads_here,), jnp.float32), zero_state),
    )[1]
    decay_before = jnp.exp(jnp.cumsum(block_ends, axis=0) - block_ends)
    span_start = decay_before[:, :, None, None] * incoming[None] + local_starts
    carried = jnp.einsum(
        "ctgn,cgjpn->ctgjp",
        c_spans.astype(jnp.float32),
        span_start.reshape(span_count, groups_here, per_group, P_SIZE, N),
        precision=highest,
    )
    outer = jnp.exp(cumulative)[..., None] * carried.reshape(span_count, SPAN, heads_here, P_SIZE)
    prefill = (
        inner_all + outer + d_skip[None, None, :, None] * x_spans.astype(jnp.float32)
    ).astype(jnp.bfloat16)
    prefill = prefill.reshape(token_count, heads_here * P_SIZE)
    last_token = prompt_len - 1
    sources = last_token // token_count
    targets = jnp.arange(seq_count, dtype=jnp.int32)
    mine = (sources == my_index)[None, :] & (owner[None, :] == targets[:, None])
    offsets = jnp.sum(jnp.where(mine, last_token[None, :] - my_index * token_count, 0), axis=1)
    positions = jnp.arange(SPAN)

    def request_state(spot):
        span_index = spot // SPAN
        offset = spot % SPAN
        x_part = lax.dynamic_index_in_dim(x_spans, span_index, 0, keepdims=False)
        b_part = lax.dynamic_index_in_dim(b_spans, span_index, 0, keepdims=False)
        cum_part = lax.dynamic_index_in_dim(cumulative, span_index, 0, keepdims=False)
        step_part = lax.dynamic_index_in_dim(step_spans, span_index, 0, keepdims=False)
        state = lax.dynamic_index_in_dim(span_start, span_index, 0, keepdims=False)
        cum_last = lax.dynamic_index_in_dim(cum_part, offset, 0, keepdims=False)
        upto = positions[:, None] <= offset
        weight = jnp.where(
            upto, jnp.exp(jnp.where(upto, cum_last[None, :] - cum_part, 0.0)) * step_part, 0.0
        )
        scaled = group_scaled(b_part, weight)
        local_sum = jnp.einsum("shp,shn->hpn", x_part, scaled, preferred_element_type=jnp.float32)
        return (jnp.exp(cum_last)[:, None, None] * state + local_sum).astype(jnp.bfloat16)

    states = blocked(request_state, (offsets,), math.gcd(4, seq_count))
    arrived = (
        lax.all_to_all(dec_x[0], "seq", split_axis=0, concat_axis=0, tiled=True),
        lax.all_to_all(dec_b[0], "seq", split_axis=0, concat_axis=0, tiled=True),
        lax.all_to_all(dec_c[0], "seq", split_axis=0, concat_axis=0, tiled=True),
        lax.all_to_all(dec_dt[0], "seq", split_axis=0, concat_axis=0, tiled=True),
    )
    present = jnp.any(mine, axis=1)
    slots = states.shape[0]
    x_values = arrived[0].reshape(slots, STEPS, heads_here, P_SIZE).astype(jnp.float32)
    b_values = arrived[1].reshape(slots, STEPS, groups_here, N)
    c_values = arrived[2].reshape(slots, STEPS, groups_here, N)
    steps_now = jax.nn.softplus(arrived[3].astype(jnp.float32))
    running = jnp.cumsum(-jnp.exp(a_log)[None, None, :] * steps_now, axis=1)
    from_state = jnp.einsum(
        "sgjpn,skgn->skgjp",
        states.reshape(slots, groups_here, per_group, P_SIZE, N),
        c_values,
        preferred_element_type=jnp.float32,
    )
    from_state = from_state.reshape(slots, STEPS, heads_here, P_SIZE)
    pair_scores = jnp.einsum(
        "skgn,slgn->sklg", c_values, b_values, preferred_element_type=jnp.float32
    )
    pair_heads = jnp.repeat(pair_scores, per_group, axis=3)
    lower = jnp.arange(STEPS)[:, None] >= jnp.arange(STEPS)[None, :]
    gaps = running[:, :, None, :] - running[:, None, :, :]
    factors = jnp.where(
        lower[None, :, :, None],
        jnp.exp(jnp.where(lower[None, :, :, None], gaps, 0.0)) * steps_now[:, None, :, :],
        0.0,
    )
    fresh = jnp.einsum("sklh,slhp->skhp", factors * pair_heads, x_values, precision=highest)
    result = (
        jnp.exp(running)[..., None] * from_state + fresh + d_skip[None, None, :, None] * x_values
    )
    result = jnp.where(present[:, None, None, None], result, 0.0)
    local_result = result.astype(jnp.bfloat16).reshape(slots, STEPS, heads_here * P_SIZE)
    decoded = lax.all_to_all(local_result, "seq", split_axis=0, concat_axis=0, tiled=True)
    return (prefill, decoded[None])


def solution(mesh):
    placed = (
        P(("grp", "seq"), "tp"),
        P(("grp", "seq"), "tp"),
        P(("grp", "seq"), "tp"),
        P(("grp", "seq"), "tp"),
        P("tp"),
        P("tp"),
        P("grp"),
        P("grp"),
        P(("grp", "seq"), None, None, "tp"),
        P(("grp", "seq"), None, None, "tp"),
        P(("grp", "seq"), None, None, "tp"),
        P(("grp", "seq"), None, None, "tp"),
    )
    return jax.shard_map(
        shards,
        mesh=mesh,
        in_specs=placed,
        out_specs=(P(("grp", "seq"), "tp"), P(("grp", "seq"), None, None, "tp")),
        check_vma=False,
    )
```

profile of v0, /device:TPU:0, one launch (start us, length us, event | category | flops | bytes accessed | tf_op | source)
XLA Modules:
  0.0 146.8 jit_solution(14673091983803329230)
XLA Ops:
  12.0 1.5 %copy.99 = bf16[256,2048]{0,1:T(8,128)(2,1)S(1)} copy(bf16[256,2048]{1,0:T(8,128)(2,1)} %param.16) | data formatting | bytes 2097152 | tf_op args[0]
  13.5 1.3 squeeze.83
  16.0 2.1 %fusion.16 = f32[2,32,64,128]{3,2,1,0:T(8,128)S(1)} fusion(f32[2,128,32,128]{3,1,2,0:T(8,128)S(1)} %bitcast.129, f32[2,128,32]{1,2,0:T(8,128)S(1)} %copy-done.12, bf16[2,128,32,64]{1,0,3,2:T(2,128)(2,1)S(1)} %copy-done.5), kind=kOutput, calls=%fused_computation.33 | convolution fusion | flops 136314880 | bytes 7372800 | tf_op jit(solution)/shard_map/while/body/eval_jaxpr/vmap(shp,shn->hpn)/dot_general | solution.py:75
  18.1 2.6 %while.8 = (s32[]{:T(128)}, f32[32,64,128]{2,1,0:T(8,128)S(1)}, f32[2,32,64,128]{3,2,1,0:T(8,128)}, f32[2,32]{1,0:T(2,128)S(1)}, f32[2,32,64,128]{3,2,1,0:T(8,128)S(1)}, /*index=5*/s32[]{:T(128)}, s32[]{:T(128)}) while((s32[]{:T(128)}, f32[32,64,128]{2,1,0:T(8,128)S(1)}, f32[2,32,64,128]{3,2,1,0:T(8,128)}, f32[2,32]{1,0:T(2,128)S(1)}, ...), condition=%wide.region_4.5_spmd.clone, body=%wide.region_3.4_spmd.clone.sunk | while | flops 1048579 | bytes 5243372 | solution.py:88
  18.1 1.1 bitcast_dynamic-update-slice_fusion.2
  19.4 1.1 bitcast_dynamic-update-slice_fusion.2
  21.8 6.4 %all-to-all-start = ((bf16[4,4,32]{2,1,0:T(4,128)(2,1)}), bf16[4,4,32]{2,1,0:T(4,128)(2,1)S(1)}, u32[]{:S(2)}, u32[]{:S(2)}) async-start(bf16[4,4,32]{2,1,0:T(4,128)(2,1)} %bitcast.14), calls=%async_computation | async-start | bytes 8192 | tf_op jit(solution)/shard_map/all_to_all | solution.py:142
  35.7 3.3 %fusion.17 = f32[2,128,32,64]{1,3,2,0:T(8,128)} fusion(f32[2,32,128,128]{3,2,1,0:T(8,128)S(1)} %bitcast.135, f32[2,32,128]{2,1,0:T(8,128)S(1)} %copy.98, f32[2,32,128]{2,1,0:T(8,128)S(1)} %copy.95, pred[128,128]{1,0:T(8,128)(4,1)S(1)} %iota_compare_fusion, bf16[2,128,32,64]{1,0,3,2:T(2,128)(2,1)S(1)} %copy-done.6), kind=kOutput, calls=%fused_computation.35 | convolution fusion | flops 140509184 | bytes 7421952 | tf_op jit(solution)/shard_map/while/body/eval_jaxpr/vmap(hts,shp->thp)/dot_general | solution.py:73
  39.7 5.1 %all-to-all-start.2 = ((bf16[4,4,256]{2,1,0:T(4,128)(2,1)}), bf16[4,4,256]{2,1,0:T(4,128)(2,1)S(1)}, u32[]{:S(2)}, u32[]{:S(2)}) async-start(bf16[4,4,256]{2,1,0:T(4,128)(2,1)} %bitcast.26), calls=%async_computation.2 | async-start | bytes 16384 | tf_op jit(solution)/shard_map/all_to_all | solution.py:140
  46.1 1.2 dynamic-slice.2
  48.9 12.6 %all-reduce.2 = f32[128]{0:T(128)S(1)} all-reduce(f32[128]{0:T(128)S(1)} %dynamic-update-slice), channel_id=2, replica_groups=mesh['grp'=2,'seq'=4,'tp'=4] {'seq'}, use_global_device_ids=true, to_apply=%add.2 | all-reduce | flops 128 | bytes 1024
  62.2 4.7 %copy.101 = f32[2,128,32,64]{1,0,3,2:T(2,128)} copy(f32[2,128,32,64]{1,3,2,0:T(8,128)} %fusion.17) | data formatting | bytes 4194304 | tf_op jit(solution)/shard_map/while/body/eval_jaxpr/vmap(hts,shp->thp)/transpose | solution.py:73
  67.6 2.2 %gather_fusion.2 = bf16[4,128,32,64]{1,3,2,0:T(8,128)(2,1)} fusion(bf16[2,128,32,64]{1,3,2,0:T(8,128)(2,1)S(1)} %copy.100, s32[4]{0:T(128)S(1)} %get-tuple-element.252), kind=kCustom, calls=%fused_computation.2 | custom fusion | bytes 4194368 | tf_op jit(solution)/shard_map/while/body/eval_jaxpr/vmap(jit(dynamic_index_in_dim))/gather | solution.py:123
  71.0 3.2 %all-to-all-start.1 = ((bf16[4,4,256]{2,1,0:T(4,128)(2,1)}), bf16[4,4,256]{2,1,0:T(4,128)(2,1)S(1)}, u32[]{:S(2)}, u32[]{:S(2)}) async-start(bf16[4,4,256]{2,1,0:T(4,128)(2,1)} %bitcast.20), calls=%async_computation.1 | async-start | bytes 16384 | tf_op jit(solution)/shard_map/all_to_all | solution.py:141
  76.6 4.0 %all-to-all-done.1 = bf16[4,4,256]{2,1,0:T(4,128)(2,1)S(1)} async-done(((bf16[4,4,256]{2,1,0:T(4,128)(2,1)}), bf16[4,4,256]{2,1,0:T(4,128)(2,1)S(1)}, u32[]{:S(2)}, u32[]{:S(2)}) %all-to-all-start.1) | async-done | bytes 8224 | tf_op jit(solution)/shard_map/all_to_all | solution.py:141
  80.6 3.5 %all-to-all-start.3 = ((bf16[4,4,2048]{2,1,0:T(4,128)(2,1)}), bf16[4,4,2048]{2,1,0:T(4,128)(2,1)S(1)}, u32[]{:S(2)}, u32[]{:S(2)}) async-start(bf16[4,4,2048]{2,1,0:T(4,128)(2,1)} %bitcast.30), calls=%async_computation.3 | async-start | bytes 131072 | tf_op jit(solution)/shard_map/all_to_all | solution.py:139
  85.6 4.5 %all-to-all-done.3 = bf16[4,4,2048]{2,1,0:T(4,128)(2,1)S(1)} async-done(((bf16[4,4,2048]{2,1,0:T(4,128)(2,1)}), bf16[4,4,2048]{2,1,0:T(4,128)(2,1)S(1)}, u32[]{:S(2)}, u32[]{:S(2)}) %all-to-all-start.3) | async-done | bytes 65568 | tf_op jit(solution)/shard_map/all_to_all | solution.py:139
  90.9 16.5 %all-gather.4.cloned.1.call-done = f32[128,64,128]{2,1,0:T(8,128)} async-done(((f32[32,64,128]{2,1,0:T(8,128)}), f32[128,64,128]{2,1,0:T(8,128)}) %all-gather.4.cloned.1.call-update) | async-done | bytes 4194320 | tf_op jit(solution)/shard_map/all_gather | solution.py:18
  107.4 4.5 %while.18 = (s32[]{:T(128)}, f32[32,64,128]{2,1,0:T(8,128)S(1)}, s32[]{:T(128)}, f32[4,32]{1,0:T(4,128)S(1)}, f32[4,32,64,128]{3,2,1,0:T(8,128)}, /*index=5*/s32[]{:T(128)}, s32[]{:T(128)}) while((s32[]{:T(128)}, f32[32,64,128]{2,1,0:T(8,128)S(1)}, s32[]{:T(128)}, f32[4,32]{1,0:T(4,128)S(1)}, f32[4,32,64,128]{3,2,1,0:T(8,128)}, ...), condition=%wide.region_6.7_spmd.clone, body=%wide.region_5.6_spmd.clone.sunk | while | flops 1048580 | bytes 3146225 | solution.py:27
  107.4 1.5 fusion.72
  108.9 1.5 fusion.72
  110.4 1.5 fusion.72
  111.9 1.8 %multiply_add_fusion = f32[2,32,64,128]{3,2,1,0:T(8,128)S(1)} fusion(f32[2,32,64,128]{3,2,1,0:T(8,128)} %get-tuple-element.180, f32[32,64,128]{2,1,0:T(8,128)S(1)} %get-tuple-element.179, f32[2,32]{1,0:T(2,128)S(1)} %copy-done.21), kind=kLoop, calls=%fused_computation.26 | loop fusion | flops 1048576 | bytes 5243136 | tf_op jit(solution)/shard_map/add | solution.py:101
  113.7 2.8 %gather_fusion.1 = f32[4,32,64,128]{3,2,1,0:T(8,128)} fusion(f32[2,32,64,128]{3,2,1,0:T(8,128)S(1)} %multiply_add_fusion, s32[4]{0:T(128)S(1)} %get-tuple-element.252), kind=kCustom, calls=%fused_computation.1 | custom fusion | bytes 8388672 | tf_op jit(solution)/shard_map/while/body/eval_jaxpr/vmap(jit(dynamic_index_in_dim))/gather | solution.py:127
  116.5 1.1 convolution_bitcast_fusion
  117.6 3.0 %copy.107 = f32[2,128,2,16,64]{1,0,4,3,2:T(2,128)} copy(f32[2,128,2,16,64]{1,4,3,2,0:T(8,128)S(1)} %convolution_bitcast_fusion) | data formatting | bytes 4194304 | tf_op jit(solution)/shard_map/ctgn,cgjpn->ctgjp/transpose | solution.py:102
  122.2 1.2 copy-done.2
  123.4 3.3 %add_convert_fusion = bf16[4,32,64,128]{3,2,1,0:T(8,128)(2,1)S(1)} fusion(f32[4,32,64,128]{3,2,1,0:T(8,128)S(1)} %copy-done.2, f32[4,32]{1,0:T(4,128)S(1)} %copy-done.20, bf16[4,128,32,64]{1,3,2,0:T(8,128)(2,1)S(1)} %copy-done.1, f32[4,128,32,128]{3,1,2,0:T(8,128)S(1)} %bitcast.128, f32[4,128,32]{1,2,0:T(8,128)S(1)} %copy-done.10), kind=kOutput, calls=%fused_computation.16 | convolution fusion | flops 275775488 | bytes 16843264 | tf_op jit(solution)/shard_map/while/body/eval_jaxpr/vmap(shp,shn->hpn)/dot_general | solution.py:134
  126.9 1.7 %fusion.45 = f32[4,2,16,64,4]{3,4,2,1,0:T(4,128)S(1)} fusion(bf16[4,2,16,64,128]{4,3,2,1,0:T(8,128)(2,1)S(1)} %bitcast.132, bf16[4,4,256]{2,1,0:T(4,128)(2,1)S(1)} %all-to-all-done.1), kind=kOutput, calls=%fused_computation.75 | convolution fusion | flops 8388608 | bytes 2236416 | tf_op jit(solution)/shard_map/sgjpn,skgn->skgjp/dot_general | solution.py:151
  130.4 3.3 %all-to-all-start.4 = ((bf16[4,4,2048]{2,1,0:T(4,128)(2,1)}), bf16[4,4,2048]{2,1,0:T(4,128)(2,1)S(1)}, u32[]{:S(2)}, u32[]{:S(2)}) async-start(bf16[4,4,2048]{2,1,0:T(4,128)(2,1)} %reshape.323), calls=%async_computation.4 | async-start | bytes 131072 | tf_op jit(solution)/shard_map/all_to_all | solution.py:175
  135.2 1.6 %fusion.9 = bf16[256,2048]{0,1:T(8,128)(2,1)} fusion(f32[256,8,2,128]{3,2,1,0:T(2,128)S(1)} %bitcast.131, f32[256,8,2,128]{3,2,1,0:T(2,128)S(1)} %bitcast.133, f32[256,8,2,128]{3,2,1,0:T(2,128)S(1)} %bitcast.130, bf16[256,2048]{0,1:T(8,128)(2,1)S(1)} %copy-done.4, f32[2048]{0:T(1024)S(1)} %copy-done.18), kind=kLoop, calls=%fused_computation.25 | loop fusion | flops 3145728 | bytes 8396800 | tf_op jit(solution)/shard_map/convert_element_type | solution.py:111
  136.8 2.3 %copy.122 = bf16[256,2048]{1,0:T(8,128)(2,1)} copy(bf16[256,2048]{0,1:T(8,128)(2,1)} %fusion.9) | data formatting | bytes 2097152
  (134 shorter events, 30.9 us)
Async XLA Ops:
  7.2 100.2 %all-gather.4.cloned.1.call-start = ((), (), s32[]{:S(2)}) async-start(), calls=%async_computation.5 | async-start | bytes 5242880 | tf_op jit(solution)/shard_map/all_gather | solution.py:18
  13.5 1.8 %copy-start.3 = (bf16[256,2048]{0,1:T(8,128)(2,1)}, bf16[256,2048]{0,1:T(8,128)(2,1)S(1)}, u32[]{:S(2)}) copy-start(bf16[256,2048]{0,1:T(8,128)(2,1)S(1)} %copy.99) | copy-start | bytes 3145732
  14.7 1.2 copy-start.12
  18.1 12.7 %copy-start.26 = (s32[8]{0:T(128)S(1)}, s32[8]{0:T(128)}, u32[]{:S(2)}) copy-start(s32[8]{0:T(128)} %param.23) | copy-start | bytes 100
  21.8 17.9 %all-to-all-start = ((bf16[4,4,32]{2,1,0:T(4,128)(2,1)}), bf16[4,4,32]{2,1,0:T(4,128)(2,1)S(1)}, u32[]{:S(2)}, u32[]{:S(2)}) async-start(bf16[4,4,32]{2,1,0:T(4,128)(2,1)} %bitcast.14), calls=%async_computation | async-start | bytes 8192 | tf_op jit(solution)/shard_map/all_to_all | solution.py:142
  34.4 1.3 copy-start.6
  35.7 3.3 %copy-start.27 = (s32[8]{0:T(128)S(1)}, s32[8]{0:T(128)}, u32[]{:S(2)}) copy-start(s32[8]{0:T(128)} %param.23) | copy-start | bytes 100
  39.0 22.5 %copy-start.9 = (f32[2,128,32]{2,1,0:T(8,128)S(1)}, f32[2,128,32]{2,1,0:T(8,128)}, u32[]{:S(2)}) copy-start(f32[2,128,32]{2,1,0:T(8,128)} %get-tuple-element.243) | copy-start | bytes 98308
  39.7 30.8 %all-to-all-start.2 = ((bf16[4,4,256]{2,1,0:T(4,128)(2,1)}), bf16[4,4,256]{2,1,0:T(4,128)(2,1)S(1)}, u32[]{:S(2)}, u32[]{:S(2)}) async-start(bf16[4,4,256]{2,1,0:T(4,128)(2,1)} %bitcast.26), calls=%async_computation.2 | async-start | bytes 16384 | tf_op jit(solution)/shard_map/all_to_all | solution.py:140
  62.2 4.7 %copy-start.24 = (f32[32]{0:T(128)S(1)}, f32[32]{0:T(128)}, u32[]{:S(2)}) copy-start(f32[32]{0:T(128)} %param.21) | copy-start | bytes 388
  67.6 6.7 %copy-start.23 = (f32[32]{0:T(128)S(1)}, f32[32]{0:T(128)}, u32[]{:S(2)}) copy-start(f32[32]{0:T(128)} %copy-done.22) | copy-start | bytes 388
  71.0 9.5 %all-to-all-start.1 = ((bf16[4,4,256]{2,1,0:T(4,128)(2,1)}), bf16[4,4,256]{2,1,0:T(4,128)(2,1)S(1)}, u32[]{:S(2)}, u32[]{:S(2)}) async-start(bf16[4,4,256]{2,1,0:T(4,128)(2,1)} %bitcast.20), calls=%async_computation.1 | async-start | bytes 16384 | tf_op jit(solution)/shard_map/all_to_all | solution.py:141
  80.6 9.5 %all-to-all-start.3 = ((bf16[4,4,2048]{2,1,0:T(4,128)(2,1)}), bf16[4,4,2048]{2,1,0:T(4,128)(2,1)S(1)}, u32[]{:S(2)}, u32[]{:S(2)}) async-start(bf16[4,4,2048]{2,1,0:T(4,128)(2,1)} %bitcast.30), calls=%async_computation.3 | async-start | bytes 131072 | tf_op jit(solution)/shard_map/all_to_all | solution.py:139
  107.4 4.5 %copy-start.21 = (f32[2,32]{1,0:T(2,128)S(1)}, f32[2,32]{1,0:T(2,128)}, u32[]{:S(2)}) copy-start(f32[2,32]{1,0:T(2,128)} %subtract_exponential_fusion) | copy-start | bytes 772
  120.6 1.6 %copy-start.1 = (bf16[4,128,32,64]{1,3,2,0:T(8,128)(2,1)S(1)}, bf16[4,128,32,64]{1,3,2,0:T(8,128)(2,1)}, u32[]{:S(2)}) copy-start(bf16[4,128,32,64]{1,3,2,0:T(8,128)(2,1)} %gather_fusion.2) | copy-start | bytes 6291460
  120.6 2.8 %copy-start.2 = (f32[4,32,64,128]{3,2,1,0:T(8,128)S(1)}, f32[4,32,64,128]{3,2,1,0:T(8,128)}, u32[]{:S(2)}) copy-start(f32[4,32,64,128]{3,2,1,0:T(8,128)} %gather_fusion.1) | copy-start | bytes 12582916
  120.6 2.8 %copy-start.10 = (f32[4,128,32]{1,2,0:T(8,128)S(1)}, f32[4,128,32]{1,2,0:T(8,128)}, u32[]{:S(2)}) copy-start(f32[4,128,32]{1,2,0:T(8,128)} %multiply_select_fusion) | copy-start | bytes 196612
  120.6 2.8 %copy-start.20 = (f32[4,32]{1,0:T(4,128)S(1)}, f32[4,32]{1,0:T(4,128)}, u32[]{:S(2)}) copy-start(f32[4,32]{1,0:T(4,128)} %exp.96) | copy-start | bytes 1540
  126.8 1.8 %copy-start.14 = (f32[4,4,4,2]{2,1,3,0:T(4,128)S(1)}, f32[4,4,4,2]{2,1,3,0:T(4,128)}, u32[]{:S(2)}) copy-start(f32[4,4,4,2]{2,1,3,0:T(4,128)} %copy.118) | copy-start | bytes 1540
  126.8 1.9 %copy-start.13 = (bf16[4,4,32,64]{3,2,1,0:T(8,128)(2,1)S(1)}, bf16[4,4,32,64]{3,2,1,0:T(8,128)(2,1)}, u32[]{:S(2)}) copy-start(bf16[4,4,32,64]{3,2,1,0:T(8,128)(2,1)} %reshape.322) | copy-start | bytes 196612
  126.8 1.9 %copy-start.15 = (f32[4,4,32]{1,2,0:T(8,128)S(1)}, f32[4,4,32]{1,2,0:T(8,128)}, u32[]{:S(2)}) copy-start(f32[4,4,32]{1,2,0:T(8,128)} %copy.115) | copy-start | bytes 6148
  126.8 1.9 %copy-start.16 = (f32[4,4,32]{1,2,0:T(8,128)S(1)}, f32[4,4,32]{1,2,0:T(8,128)}, u32[]{:S(2)}) copy-start(f32[4,4,32]{1,2,0:T(8,128)} %copy.117) | copy-start | bytes 6148
  126.8 1.9 %copy-start.17 = (f32[4,4,32]{1,2,0:T(8,128)S(1)}, f32[4,4,32]{1,2,0:T(8,128)}, u32[]{:S(2)}) copy-start(f32[4,4,32]{1,2,0:T(8,128)} %copy.109) | copy-start | bytes 6148
  126.8 1.9 %copy-start.25 = (f32[32]{0:T(128)S(1)}, f32[32]{0:T(128)}, u32[]{:S(2)}) copy-start(f32[32]{0:T(128)} %param.21) | copy-start | bytes 388
  126.8 1.8 %copy-start.28 = (pred[4]{0:T(512)(128)(4,1)S(1)}, pred[4]{0:T(512)(128)(4,1)}, u32[]{:S(2)}) copy-start(pred[4]{0:T(512)(128)(4,1)} %fusion.50) | copy-start | bytes 16
  126.9 1.8 %copy-start.29 = (pred[4,4]{1,0:T(4,128)(4,1)S(1)}, pred[4,4]{1,0:T(4,128)(4,1)}, u32[]{:S(2)}) copy-start(pred[4,4]{1,0:T(4,128)(4,1)} %iota_compare_fusion.1) | copy-start | bytes 52
  128.6 5.1 %copy-start.11 = (f32[2,128,32]{1,0,2:T(2,128)S(1)}, f32[2,128,32]{1,0,2:T(2,128)}, u32[]{:S(2)}) copy-start(f32[2,128,32]{1,0,2:T(2,128)} %copy.102) | copy-start | bytes 98308
  128.7 5.5 %copy-start.4 = (bf16[256,2048]{0,1:T(8,128)(2,1)S(1)}, bf16[256,2048]{0,1:T(8,128)(2,1)}, u32[]{:S(2)}) copy-start(bf16[256,2048]{0,1:T(8,128)(2,1)} %copy-done.3) | copy-start | bytes 3145732
  128.7 5.5 %copy-start.7 = (f32[2,128,32,64]{1,0,3,2:T(2,128)S(1)}, f32[2,128,32,64]{1,0,3,2:T(2,128)}, u32[]{:S(2)}) copy-start(f32[2,128,32,64]{1,0,3,2:T(2,128)} %copy.101) | copy-start | bytes 6291460
  128.7 5.5 %copy-start.18 = (f32[2048]{0:T(1024)S(1)}, f32[2048]{0:T(1024)}, u32[]{:S(2)}) copy-start(f32[2048]{0:T(1024)} %mul.220) | copy-start | bytes 24580
  130.4 9.0 %all-to-all-start.4 = ((bf16[4,4,2048]{2,1,0:T(4,128)(2,1)}), bf16[4,4,2048]{2,1,0:T(4,128)(2,1)S(1)}, u32[]{:S(2)}, u32[]{:S(2)}) async-start(bf16[4,4,2048]{2,1,0:T(4,128)(2,1)} %reshape.323), calls=%async_computation.4 | async-start | bytes 131072 | tf_op jit(solution)/shard_map/all_to_all | solution.py:175
  133.6 1.6 %copy-start.8 = (f32[2,128,2,16,64]{1,0,4,3,2:T(2,128)S(1)}, f32[2,128,2,16,64]{1,0,4,3,2:T(2,128)}, u32[]{:S(2)}) copy-start(f32[2,128,2,16,64]{1,0,4,3,2:T(2,128)} %copy.107) | copy-start | bytes 6291460
  (4 other events, 3.7 us)
Sparse Core Ops, SparseCore 0:
  21.9 85.4 all-gather.3
where the time goes:
time: 148 us; the launch traced here: 147 us
  local copies, waits for them, and re-layouts  41.4 us (28%)
  waiting for transfers between devices  25.2 us (17%)
  starting transfers between devices  21.5 us (15%)
  other arithmetic  17.5 us (12%)
  between operations  15.2 us (10%)
  matrix products  13.3 us (9%)
  blocking collectives  12.6 us (9%)
    all_gather x1, waiting for transfers between devices, carried_in(): pieces = jax.tree.map(lambda part: lax.all_gather(part, axis), value)  16.5 us
    unnamed x1, blocking collectives  12.6 us
    unnamed x66, local copies, waits for them, and re-layouts  12.4 us
    all_to_all x1, starting transfers between devices, shards(): lax.all_to_all(dec_dt[0], 'seq', split_axis=0, concat_axis=0, tiled=True)  6.35 us
    all_to_all x1, starting transfers between devices, shards(): lax.all_to_all(dec_b[0], 'seq', split_axis=0, concat_axis=0, tiled=True)  5.07 us
    transpose x1, local copies, waits for them, and re-layouts, span_local(): jnp.einsum('hts,shp->thp', weights, x_part, preferred_element_type=jnp.fl...  4.67 us
    all_to_all x1, waiting for transfers between devices, shards(): lax.all_to_all(dec_x[0], 'seq', split_axis=0, concat_axis=0, tiled=True)  4.48 us
    select_n x3, other arithmetic, lap(): jnp.where(position < mine, new, old)  4.38 us
  transfers between devices with their start and end apart: 6, of which 4 were waited for; matrix products, arithmetic and copies ran while one was open for 22% of the time, Pallas kernels for 0%

commit v1 on v0

v1 whole, which is shorter than its diff:
```python
import functools

import jax
import jax.numpy as jnp
from jax import lax
from jax.experimental import pallas as pl
from jax.experimental.pallas import tpu as pltpu
from jax.sharding import PartitionSpec as P

H = 128
P_SIZE = 64
N = 128
G = 8
SPAN = 128
STEPS = 4
LANES = 256
MESH = pl.DeviceIdType.MESH
F32 = jnp.float32
BF16 = jnp.bfloat16
FAR = -1e30


def iota(shape, axis):
    return lax.broadcasted_iota(jnp.int32, shape, axis)


def dot(a, b):
    return jnp.dot(a, b, preferred_element_type=F32)


def dot_t(a, b):
    return lax.dot_general(a, b, (((1,), (1,)), ((), ())), preferred_element_type=F32)


def halves(value, count):
    pieces = []
    for _ in range(count):
        piece = value.astype(BF16)
        pieces.append(piece)
        value = value - piece.astype(F32)
    return pieces


def picked(selector, value, count=3):
    parts = [dot(selector, piece) for piece in halves(value, count)]
    return sum(parts[1:], parts[0])


def spread(pieces, expand):
    parts = [dot(piece, expand) for piece in pieces]
    return sum(parts[1:], parts[0])


def ones(mask):
    return jnp.where(mask, 1.0, 0.0).astype(BF16)


def softplus(value):
    return jnp.maximum(value, 0.0) + jnp.log1p(jnp.exp(-jnp.abs(value)))


def kernel(
    seq_count,
    x_ref, b_ref, c_ref, dt_ref, alog_ref, skip_ref, len_ref, own_ref,
    dx_ref, db_ref, dc_ref, ddt_ref,
    out_ref, dout_ref,
    rx, rb, rc, rdt, xd, bd, cd, dtd, res, dres, rres,
    inbuf, outbuf, first, total,
    send_in, recv_in, own_sem, send_state, recv_state, send_out, recv_out,
):
    me = lax.axis_index("seq")
    tokens, width = x_ref.shape
    heads = dt_ref.shape[1]
    groups = b_ref.shape[1] // N
    per_group = heads // groups
    spans = tokens // SPAN
    chunks = width // LANES
    heads_chunk = LANES // P_SIZE
    rows = seq_count * STEPS

    barrier = pltpu.get_barrier_semaphore()
    for d in range(1, seq_count):
        pl.semaphore_signal(
            barrier, inc=1, device_id={"seq": lax.rem(me + d, seq_count)}, device_id_type=MESH
        )
    pl.semaphore_wait(barrier, seq_count - 1)

    def exchange(source, landing, sends, recvs):
        copies = []
        for d in range(1, seq_count):
            target = lax.rem(me + d, seq_count)
            copies.append(
                pltpu.make_async_remote_copy(
                    src_ref=source.at[target],
                    dst_ref=landing.at[me],
                    send_sem=sends.at[d],
                    recv_sem=recvs.at[d],
                    device_id={"seq": target},
                    device_id_type=MESH,
                )
            )
        for copy in copies:
            copy.start()
        return copies

    arriving = []
    for k, (source, landing) in enumerate(
        ((dx_ref, rx), (db_ref, rb), (dc_ref, rc), (ddt_ref, rdt))
    ):
        arriving += exchange(source.at[0], landing, send_in.at[k], recv_in.at[k])
        mine_copy = pltpu.make_async_copy(source.at[0, me], landing.at[me], own_sem.at[k])
        mine_copy.start()
        arriving.append(mine_copy)

    step = softplus(dt_ref[...].astype(F32))
    rate = -jnp.exp(alog_ref[...])
    t_row, t_col = iota((tokens, tokens), 0), iota((tokens, tokens), 1)
    same = (t_row // SPAN) == (t_col // SPAN)
    cum = picked(ones(same & (t_col <= t_row)), rate * step)
    last = [cum[(s + 1) * SPAN - 1:(s + 1) * SPAN, :] for s in range(spans)]
    into = jnp.concatenate(
        [
            jnp.exp(last[s] - cum[s * SPAN:(s + 1) * SPAN]) * step[s * SPAN:(s + 1) * SPAN]
            for s in range(spans)
        ],
        axis=0,
    )
    into_parts = halves(into, 2)
    grown = [halves(jnp.exp(last[s]), 2) for s in range(spans)]
    outer_parts = halves(jnp.exp(cum), 2)
    cum_t = cum.T
    step_t = step.T

    def expander(chunk):
        return ones(iota((heads, LANES), 0) == iota((heads, LANES), 1) // P_SIZE + chunk * heads_chunk)

    def lanes(chunk):
        return slice(chunk * LANES, (chunk + 1) * LANES)

    b_t = [
        [b_ref[s * SPAN:(s + 1) * SPAN, g * N:(g + 1) * N].T for g in range(groups)]
        for s in range(spans)
    ]

    def onward(chunk):
        return pltpu.make_async_remote_copy(
            src_ref=outbuf.at[chunk],
            dst_ref=inbuf.at[chunk],
            send_sem=send_state.at[chunk],
            recv_sem=recv_state.at[chunk],
            device_id={"seq": lax.rem(me + 1, seq_count)},
            device_id_type=MESH,
        )

    for chunk in range(chunks):
        g = chunk * heads_chunk // per_group
        expand = expander(chunk)
        weighted = (x_ref[:, lanes(chunk)].astype(F32) * spread(into_parts, expand)).astype(BF16)
        state = None
        for s in range(spans):
            own = dot(b_t[s][g], weighted[s * SPAN:(s + 1) * SPAN])
            state = own if state is None else spread(grown[s], expand) * state + own
            if s < spans - 1:
                first[s, :, lanes(chunk)] = state
        total[:, lanes(chunk)] = state

        @pl.when(me == 0)
        def _():
            outbuf[chunk] = state.astype(BF16)
            inbuf[chunk] = jnp.zeros(inbuf.shape[1:], BF16)
            if seq_count > 1:
                onward(chunk).start()

    for copy in arriving:
        copy.wait()
    for q in range(seq_count):
        part = pl.ds(q * STEPS, STEPS)
        xd[part, :] = rx[q].astype(F32)
        bd[part, :] = rb[q].astype(F32)
        cd[part, :] = rc[q].astype(F32)
        dtd[part, :] = rdt[q].astype(F32)
    requests = len_ref.shape[1]
    final = len_ref[...] - 1
    here = (final >= me * tokens) & (final < (me + 1) * tokens)
    chosen = here & (own_ref[...] == iota((rows, requests), 0) // STEPS)
    spot = jnp.sum(jnp.where(chosen, final - me * tokens, 0), axis=1, keepdims=True)
    present = jnp.sum(jnp.where(chosen, 1, 0), axis=1, keepdims=True) > 0
    place = iota((rows, tokens), 1)
    upto = (place <= spot) & (place // SPAN == spot // SPAN)
    cum_spot = picked(ones(place == spot), cum)
    spot_span = spot // SPAN
    spot_parts = halves(jnp.exp(cum_spot), 2)
    dstep = softplus(dtd[...])
    r_row, r_col = iota((rows, rows), 0), iota((rows, rows), 1)
    slot = (r_row // STEPS) == (r_col // STEPS)
    running = picked(ones(slot & (r_col <= r_row)), rate * dstep)
    running_parts = halves(jnp.exp(running), 2)
    c_dec = cd[...].astype(BF16)
    b_dec = bd[...].astype(BF16)
    x_dec = xd[...].astype(BF16)
    head_group = iota((rows, heads), 1) // per_group
    pairs = [
        dot_t(c_dec[:, g * N:(g + 1) * N], b_dec[:, g * N:(g + 1) * N]) for g in range(groups)
    ]
    step_row = iota((rows, heads), 0) % STEPS
    fresh_parts, fresh_pick = [], []
    for k in range(STEPS):
        chosen_k = slot & (r_col % STEPS == k)
        pick = ones(chosen_k)
        score = jnp.zeros((rows, heads), F32)
        for g in range(groups):
            value = jnp.sum(jnp.where(chosen_k, pairs[g], 0.0), axis=1, keepdims=True)
            score = jnp.where(head_group == g, value, score)
        gap = jnp.where(step_row >= k, running - picked(pick, running), FAR)
        fresh_parts.append(halves(jnp.exp(gap) * picked(pick, dstep) * score, 2))
        fresh_pick.append(pick)
    skip_parts = halves(skip_ref[...], 3)

    scores, dec_scores = [], []
    for s in range(spans):
        at = slice(s * SPAN, (s + 1) * SPAN)
        scores.append([])
        dec_scores.append([])
        for g in range(groups):
            cols = slice(g * N, (g + 1) * N)
            scores[s].append(dot_t(c_ref[at, cols], b_ref[at, cols]))
            dec_scores[s].append(dot_t(c_dec[:, cols], b_ref[at, cols]))
    causal = iota((SPAN, SPAN), 0) >= iota((SPAN, SPAN), 1)
    low = ones(iota((1, 2 * P_SIZE), 1) < P_SIZE)
    high = ones(iota((1, 2 * P_SIZE), 1) >= P_SIZE)

    def weights(head, s):
        g = head // per_group
        at = slice(s * SPAN, (s + 1) * SPAN)
        row = cum_t[head:head + 1, at]
        size = step_t[head:head + 1, at]
        gap = jnp.where(causal, cum[at, head:head + 1] - row, FAR)
        main = scores[s][g] * jnp.exp(gap) * size
        gap = jnp.where(upto[:, at], cum_spot[:, head:head + 1] - row, FAR)
        extra = dec_scores[s][g] * jnp.exp(gap) * size
        return jnp.concatenate([main.astype(BF16), extra.astype(BF16)], axis=0)

    for chunk in range(chunks):
        g = chunk * heads_chunk // per_group
        cols = slice(g * N, (g + 1) * N)
        expand = expander(chunk)
        grow = [spread(grown[s], expand) for s in range(spans)]
        if seq_count > 1:

            @pl.when(me > 0)
            def _():
                onward(chunk).wait_recv()

            @pl.when((me > 0) & (me < seq_count - 1))
            def _():
                through = grow[0]
                for s in range(1, spans):
                    through = through * grow[s]
                outbuf[chunk] = (
                    through * inbuf[chunk].astype(F32) + total[:, lanes(chunk)]
                ).astype(BF16)
                onward(chunk).start()

        incoming = inbuf[chunk]
        outer = spread(outer_parts, expand)
        skip = spread(skip_parts, expand)
        from_block = None
        from_carried = None
        reach = incoming.astype(F32)
        passed = None
        for s in range(spans):
            at = slice(s * SPAN, (s + 1) * SPAN)
            inner = []
            for pair in range(heads_chunk // 2):
                head = chunk * heads_chunk + 2 * pair
                start = chunk * LANES + pair * 2 * P_SIZE
                x_pair = x_ref[at, start:start + 2 * P_SIZE]
                both = jnp.concatenate([x_pair * low, x_pair * high], axis=0)
                left = jnp.concatenate([weights(head, s), weights(head + 1, s)], axis=1)
                inner.append(dot(left, both))
            inner = jnp.concatenate(inner, axis=1)
            if s == 0:
                held = incoming
            else:
                passed = grow[s - 1] if passed is None else passed * grow[s - 1]
                held = (passed * reach + first[s - 1, :, lanes(chunk)]).astype(BF16)
            carried = dot(jnp.concatenate([c_ref[at, cols], c_dec[:, cols]], axis=0), held)
            x_part = x_ref[at, lanes(chunk)].astype(F32)
            out_ref[at, lanes(chunk)] = (
                inner[:SPAN] + outer[at] * carried[:SPAN] + skip * x_part
            ).astype(BF16)
            from_block = inner[SPAN:] if s == 0 else from_block + inner[SPAN:]
            from_carried = (
                carried[SPAN:]
                if s == 0
                else jnp.where(spot_span == s, carried[SPAN:], from_carried)
            )
        state_part = spread(spot_parts, expand) * from_carried + from_block
        xd_part = x_dec[:, lanes(chunk)]
        value = spread(running_parts, expand) * state_part + skip * xd_part.astype(F32)
        for k in range(STEPS):
            value = value + spread(fresh_parts[k], expand) * dot(fresh_pick[k], xd_part)
        res[:, lanes(chunk)] = jnp.where(present, value, 0.0)

    for q in range(seq_count):
        dres[q] = res[pl.ds(q * STEPS, STEPS), :].astype(BF16)
    leaving = exchange(dres, rres, send_out, recv_out)
    mine_copy = pltpu.make_async_copy(dres.at[me], rres.at[me], own_sem.at[0])
    mine_copy.start()
    for copy in leaving + [mine_copy]:
        copy.wait()
    dout_ref[0] = rres[...]
    if seq_count > 1:

        @pl.when(me < seq_count - 1)
        def _():
            for chunk in range(chunks):
                onward(chunk).wait_send()


def shards(
    ssm_input, bmat, cmat, dt_raw, a_log, d_skip, prompt_len, owner, dec_x, dec_b, dec_c, dec_dt
):
    seq_count = lax.axis_size("seq")
    tokens, width = ssm_input.shape
    heads = dt_raw.shape[1]
    gn = bmat.shape[1]
    spans = tokens // SPAN
    chunks = width // LANES
    rows = seq_count * STEPS
    vmem = pl.BlockSpec(memory_space=pltpu.VMEM)
    dma = pltpu.SemaphoreType.DMA
    slots = (seq_count, STEPS)
    return pl.pallas_call(
        functools.partial(kernel, seq_count),
        out_shape=(
            jax.ShapeDtypeStruct((tokens, width), BF16),
            jax.ShapeDtypeStruct((1,) + slots + (width,), BF16),
        ),
        in_specs=[vmem] * 12,
        out_specs=(vmem, vmem),
        scratch_shapes=[
            pltpu.VMEM(slots + (width,), BF16),
            pltpu.VMEM(slots + (gn,), BF16),
            pltpu.VMEM(slots + (gn,), BF16),
            pltpu.VMEM(slots + (heads,), BF16),
            pltpu.VMEM((rows, width), F32),
            pltpu.VMEM((rows, gn), F32),
            pltpu.VMEM((rows, gn), F32),
            pltpu.VMEM((rows, heads), F32),
            pltpu.VMEM((rows, width), F32),
            pltpu.VMEM(slots + (width,), BF16),
            pltpu.VMEM(slots + (width,), BF16),
            pltpu.VMEM((chunks, N, LANES), BF16),
            pltpu.VMEM((chunks, N, LANES), BF16),
            pltpu.VMEM((max(spans - 1, 1), N, width), F32),
            pltpu.VMEM((N, width), F32),
            dma((4, seq_count)),
            dma((4, seq_count)),
            dma((4,)),
            dma((chunks,)),
            dma((chunks,)),
            dma((seq_count,)),
            dma((seq_count,)),
        ],
        compiler_params=pltpu.CompilerParams(
            collective_id=0, has_side_effects=True, vmem_limit_bytes=40 * 1024 * 1024
        ),
    )(
        ssm_input, bmat, cmat, dt_raw, a_log[None, :], d_skip[None, :],
        prompt_len[None, :], owner[None, :], dec_x, dec_b, dec_c, dec_dt,
    )


def solution(mesh):
    placed = (
        P(("grp", "seq"), "tp"),
        P(("grp", "seq"), "tp"),
        P(("grp", "seq"), "tp"),
        P(("grp", "seq"), "tp"),
        P("tp"),
        P("tp"),
        P("grp"),
        P("grp"),
        P(("grp", "seq"), None, None, "tp"),
        P(("grp", "seq"), None, None, "tp"),
        P(("grp", "seq"), None, None, "tp"),
        P(("grp", "seq"), None, None, "tp"),
    )
    return jax.shard_map(
        shards,
        mesh=mesh,
        in_specs=placed,
        out_specs=(P(("grp", "seq"), "tp"), P(("grp", "seq"), None, None, "tp")),
        check_vma=False,
    )
```

time: 148 us -> 38.7 us (0.26)
  local copies, waits for them, and re-layouts: 41.4 us -> 5.56 us
  Pallas kernels: 0 us -> 32.2 us
  waiting for transfers between devices: 25.2 us -> 0 us
  starting transfers between devices: 21.5 us -> 0 us
  other arithmetic: 17.5 us -> 0 us
  between operations: 15.2 us -> 0.78 us
  matrix products: 13.3 us -> 0 us
  blocking collectives: 12.6 us -> 0 us
    pallas_call x0 -> x1, Pallas kernels: none -> 32.2 us  [shards(): pl.pallas_call(functools.partial(kernel, seq_count), out_shape=(jax.Shape...]
    all_to_all x5 -> x0, starting transfers between devices: 21.4 us -> none  [the longest x1 6.35 us: shards(): lax.all_to_all(dec_dt[0], 'seq', split_axis=0, concat_axis=0, tiled=True)]
    all_gather x1 -> x0, waiting for transfers between devices: 16.5 us -> none  [carried_in(): pieces = jax.tree.map(lambda part: lax.all_gather(part, axis), value)]
    dot_general x8 -> x0, matrix products: 13.3 us -> none  [the longest x1 3.34 us: request_state(): jnp.einsum('shp,shn->hpn', x_part, scaled, preferred_element_type=jnp.flo...]
    unnamed x1 -> x0, blocking collectives: 12.6 us -> none
    all_to_all x5 -> x0, waiting for transfers between devices: 8.76 us -> none  [the longest x1 4.48 us: shards(): lax.all_to_all(dec_x[0], 'seq', split_axis=0, concat_axis=0, tiled=True)]
    transpose x5 -> x0, local copies, waits for them, and re-layouts: 8.56 us -> none  [the longest x1 4.67 us: span_local(): jnp.einsum('hts,shp->thp', weights, x_part, preferred_element_type=jnp.fl...]
    gather x7 -> x0, local copies, waits for them, and re-layouts: 7.42 us -> none  [the longest x1 2.78 us: request_state(): state = lax.dynamic_index_in_dim(span_start, span_index, 0, keepdims=False)]
  transfers between devices with their start and end apart: 6 -> 0, of which waited for: 4 -> 0; matrix products, arithmetic and copies ran while one was open for 22% -> 0% of each run, Pallas kernels for 0% -> 0%
where the time goes in v1:
time: 38.7 us; the launch traced here: 38.5 us
  Pallas kernels  32.2 us (83%)
  local copies, waits for them, and re-layouts  5.56 us (14%)
  between operations  0.78 us (2%)
    pallas_call x1, Pallas kernels, shards(): pl.pallas_call(functools.partial(kernel, seq_count), out_shape=(jax.Shape...  32.2 us
    unnamed x25, local copies, waits for them, and re-layouts  5.56 us

profile of v1, /device:TPU:0, one launch (start us, length us, event | category | flops | bytes accessed | tf_op | source)
XLA Modules:
  0.0 38.5 jit_solution(7324193778188100180)
XLA Ops:
  0.6 0.0 copy-start.3
  0.6 0.0 copy-start.4
  0.7 0.0 copy-start.5
  0.7 0.0 copy-start.6
  0.7 0.0 copy-start.7
  0.7 0.0 copy-start.8
  0.7 0.0 copy-start.9
  0.7 0.0 copy-start.10
  0.7 0.9 %copy.14.dt_ref = bf16[256,32]{1,0:T(8,128)(2,1)S(1)} copy(bf16[256,32]{0,1:T(8,128)(2,1)} %param.15) | data formatting | bytes 32768 | tf_op args[3]
  1.6 0.0 copy-done.3
  1.6 0.0 copy-done.4
  1.6 0.0 copy-done.5
  1.6 0.0 copy-done.6
  1.6 0.0 copy-done.7
  1.7 0.0 copy-done.8
  1.7 0.0 copy-done.9
  1.7 0.0 copy-done.10
  1.7 0.0 copy-start
  1.7 1.2 %copy-done = bf16[256,2048]{1,0:T(8,128)(2,1)S(1)} copy-done((bf16[256,2048]{1,0:T(8,128)(2,1)S(1)}, bf16[256,2048]{1,0:T(8,128)(2,1)}, u32[]{:S(2)}) %copy-start) | copy-done | bytes 1048600
  2.9 0.0 copy-start.1
  2.9 0.9 %copy-done.1 = bf16[256,256]{1,0:T(8,128)(2,1)S(1)} copy-done((bf16[256,256]{1,0:T(8,128)(2,1)S(1)}, bf16[256,256]{1,0:T(8,128)(2,1)}, u32[]{:S(2)}) %copy-start.1) | copy-done | bytes 131096
  3.8 0.0 copy-start.2
  3.8 0.9 %copy-done.2 = bf16[256,256]{1,0:T(8,128)(2,1)S(1)} copy-done((bf16[256,256]{1,0:T(8,128)(2,1)S(1)}, bf16[256,256]{1,0:T(8,128)(2,1)}, u32[]{:S(2)}) %copy-start.2) | copy-done | bytes 131096
  4.7 32.2 %shard_map.131 = (bf16[256,2048]{1,0:T(8,128)(2,1)S(1)}, bf16[1,4,4,2048]{3,2,1,0:T(4,128)(2,1)S(1)}) custom-call(bf16[256,2048]{1,0:T(8,128)(2,1)S(1)} %copy-done, bf16[256,256]{1,0:T(8,128)(2,1)S(1)} %copy-done.1, bf16[256,256]{1,0:T(8,128)(2,1)S(1)} %copy-done.2, bf16[256,32]{1,0:T(8,128)(2,1)S(1)} %copy.14.dt_ref, f32[1,32]{1,0:T(1,128)S(1)} %bitcast.4, ...), custom_call_target="tpu_custom_call" | custom-call | tf_op jit(solution)/shard_map/pallas_call | solution.py:334
  36.9 1.0 %copy.17 = bf16[256,2048]{1,0:T(8,128)(2,1)} copy(bf16[256,2048]{1,0:T(8,128)(2,1)S(1)} %get-tuple-element.4) | data formatting | bytes 2097152
  37.9 0.6 %copy.18 = bf16[1,4,4,2048]{3,2,1,0:T(4,128)(2,1)} copy(bf16[1,4,4,2048]{3,2,1,0:T(4,128)(2,1)S(1)} %get-tuple-element.5) | data formatting | bytes 131072
Async XLA Ops:
  0.6 1.0 %copy-start.3 = (bf16[1,4,4,2048]{3,2,1,0:T(4,128)(2,1)S(1)}, bf16[1,4,4,2048]{3,2,1,0:T(4,128)(2,1)}, u32[]{:S(2)}) copy-start(bf16[1,4,4,2048]{3,2,1,0:T(4,128)(2,1)} %dx_ref.1) | copy-start | bytes 196612
  0.6 1.0 %copy-start.4 = (bf16[1,4,4,256]{3,2,1,0:T(4,128)(2,1)S(1)}, bf16[1,4,4,256]{3,2,1,0:T(4,128)(2,1)}, u32[]{:S(2)}) copy-start(bf16[1,4,4,256]{3,2,1,0:T(4,128)(2,1)} %db_ref.1) | copy-start | bytes 24580
  0.7 1.0 %copy-start.5 = (bf16[1,4,4,256]{3,2,1,0:T(4,128)(2,1)S(1)}, bf16[1,4,4,256]{3,2,1,0:T(4,128)(2,1)}, u32[]{:S(2)}) copy-start(bf16[1,4,4,256]{3,2,1,0:T(4,128)(2,1)} %dc_ref.1) | copy-start | bytes 24580
  0.7 1.0 %copy-start.6 = (bf16[1,4,4,32]{3,2,1,0:T(4,128)(2,1)S(1)}, bf16[1,4,4,32]{3,2,1,0:T(4,128)(2,1)}, u32[]{:S(2)}) copy-start(bf16[1,4,4,32]{3,2,1,0:T(4,128)(2,1)} %ddt_ref.1) | copy-start | bytes 3076
  0.7 1.0 %copy-start.7 = (f32[32]{0:T(128)S(1)}, f32[32]{0:T(128)}, u32[]{:S(2)}) copy-start(f32[32]{0:T(128)} %param.16) | copy-start | bytes 388
  0.7 1.0 %copy-start.8 = (f32[32]{0:T(128)S(1)}, f32[32]{0:T(128)}, u32[]{:S(2)}) copy-start(f32[32]{0:T(128)} %param.17) | copy-start | bytes 388
  0.7 1.0 %copy-start.9 = (s32[8]{0:T(128)S(1)}, s32[8]{0:T(128)}, u32[]{:S(2)}) copy-start(s32[8]{0:T(128)} %param.18) | copy-start | bytes 100
  0.7 1.0 %copy-start.10 = (s32[8]{0:T(128)S(1)}, s32[8]{0:T(128)}, u32[]{:S(2)}) copy-start(s32[8]{0:T(128)} %param.19) | copy-start | bytes 100
  1.7 1.2 %copy-start = (bf16[256,2048]{1,0:T(8,128)(2,1)S(1)}, bf16[256,2048]{1,0:T(8,128)(2,1)}, u32[]{:S(2)}) copy-start(bf16[256,2048]{1,0:T(8,128)(2,1)} %x_ref.1) | copy-start | bytes 3145732
  2.9 0.9 %copy-start.1 = (bf16[256,256]{1,0:T(8,128)(2,1)S(1)}, bf16[256,256]{1,0:T(8,128)(2,1)}, u32[]{:S(2)}) copy-start(bf16[256,256]{1,0:T(8,128)(2,1)} %b_ref.1) | copy-start | bytes 393220
  3.8 0.9 %copy-start.2 = (bf16[256,256]{1,0:T(8,128)(2,1)S(1)}, bf16[256,256]{1,0:T(8,128)(2,1)}, u32[]{:S(2)}) copy-start(bf16[256,256]{1,0:T(8,128)(2,1)} %c_ref.1) | copy-start | bytes 393220

commit v2 on v1

--- a/solution.py
+++ b/solution.py
@@ -14,6 +14,7 @@
 SPAN = 128
 STEPS = 4
 LANES = 256
+HOP = 128
 MESH = pl.DeviceIdType.MESH
 F32 = jnp.float32
 BF16 = jnp.bfloat16
@@ -61,16 +62,16 @@
 
 def kernel(
     seq_count,
-    x_ref, b_ref, c_ref, dt_ref, alog_ref, skip_ref, len_ref, own_ref,
+    x_hbm, b_hbm, c_hbm, dt_ref, alog_ref, skip_ref, len_ref, own_ref,
     dx_ref, db_ref, dc_ref, ddt_ref,
     out_ref, dout_ref,
-    rx, rb, rc, rdt, xd, bd, cd, dtd, res, dres, rres,
+    x_ref, b_ref, c_ref, rx, rb, rc, rdt, xd, bd, cd, dtd, res, dres, rres,
     inbuf, outbuf, first, total,
-    send_in, recv_in, own_sem, send_state, recv_state, send_out, recv_out,
+    load_sem, send_in, recv_in, own_sem, send_state, recv_state, send_out, recv_out,
 ):
     me = lax.axis_index("seq")
     tokens, width = x_ref.shape
-    heads = dt_ref.shape[1]
+    heads = dt_ref.shape[0]
     groups = b_ref.shape[1] // N
     per_group = heads // groups
     spans = tokens // SPAN
@@ -83,7 +84,31 @@
         pl.semaphore_signal(
             barrier, inc=1, device_id={"seq": lax.rem(me + d, seq_count)}, device_id_type=MESH
         )
-    pl.semaphore_wait(barrier, seq_count - 1)
+    loads = [
+        pltpu.make_async_copy(source, landing, load_sem.at[k])
+        for k, (source, landing) in enumerate(((x_hbm, x_ref), (b_hbm, b_ref), (c_hbm, c_ref)))
+    ]
+    for copy in loads:
+        copy.start()
+
+    step_t = softplus(dt_ref[...].astype(F32))
+    step = step_t.T
+    rate = -jnp.exp(alog_ref[...])
+    t_row, t_col = iota((tokens, tokens), 0), iota((tokens, tokens), 1)
+    same = (t_row // SPAN) == (t_col // SPAN)
+    cum = picked(ones(same & (t_col <= t_row)), rate * step)
+    last = [cum[(s + 1) * SPAN - 1:(s + 1) * SPAN, :] for s in range(spans)]
+    into = jnp.concatenate(
+        [
+            jnp.exp(last[s] - cum[s * SPAN:(s + 1) * SPAN]) * step[s * SPAN:(s + 1) * SPAN]
+            for s in range(spans)
+        ],
+        axis=0,
+    )
+    into_parts = halves(into, 2)
+    grown = [halves(jnp.exp(last[s]), 2) for s in range(spans)]
+    outer_parts = halves(jnp.exp(cum), 2)
+    cum_t = cum.T
 
     def exchange(source, landing, sends, recvs):
         copies = []
@@ -103,51 +128,30 @@
             copy.start()
         return copies
 
-    arriving = []
-    for k, (source, landing) in enumerate(
-        ((dx_ref, rx), (db_ref, rb), (dc_ref, rc), (ddt_ref, rdt))
-    ):
-        arriving += exchange(source.at[0], landing, send_in.at[k], recv_in.at[k])
-        mine_copy = pltpu.make_async_copy(source.at[0, me], landing.at[me], own_sem.at[k])
-        mine_copy.start()
-        arriving.append(mine_copy)
-
-    step = softplus(dt_ref[...].astype(F32))
-    rate = -jnp.exp(alog_ref[...])
-    t_row, t_col = iota((tokens, tokens), 0), iota((tokens, tokens), 1)
-    same = (t_row // SPAN) == (t_col // SPAN)
-    cum = picked(ones(same & (t_col <= t_row)), rate * step)
-    last = [cum[(s + 1) * SPAN - 1:(s + 1) * SPAN, :] for s in range(spans)]
-    into = jnp.concatenate(
-        [
-            jnp.exp(last[s] - cum[s * SPAN:(s + 1) * SPAN]) * step[s * SPAN:(s + 1) * SPAN]
-            for s in range(spans)
-        ],
-        axis=0,
-    )
-    into_parts = halves(into, 2)
-    grown = [halves(jnp.exp(last[s]), 2) for s in range(spans)]
-    outer_parts = halves(jnp.exp(cum), 2)
-    cum_t = cum.T
-    step_t = step.T
-
     def expander(chunk):
         return ones(iota((heads, LANES), 0) == iota((heads, LANES), 1) // P_SIZE + chunk * heads_chunk)
 
     def lanes(chunk):
         return slice(chunk * LANES, (chunk + 1) * LANES)
 
+    for copy in loads:
+        copy.wait()
+    pl.semaphore_wait(barrier, seq_count - 1)
     b_t = [
         [b_ref[s * SPAN:(s + 1) * SPAN, g * N:(g + 1) * N].T for g in range(groups)]
         for s in range(spans)
     ]
-
-    def onward(chunk):
+    hops = width // HOP
+
+    def hop_lanes(hop):
+        return slice(hop * HOP, (hop + 1) * HOP)
+
+    def onward(hop):
         return pltpu.make_async_remote_copy(
-            src_ref=outbuf.at[chunk],
-            dst_ref=inbuf.at[chunk],
-            send_sem=send_state.at[chunk],
-            recv_sem=recv_state.at[chunk],
+            src_ref=outbuf.at[hop],
+            dst_ref=inbuf.at[hop],
+            send_sem=send_state.at[hop],
+            recv_sem=recv_state.at[hop],
             device_id={"seq": lax.rem(me + 1, seq_count)},
             device_id_type=MESH,
         )
@@ -166,10 +170,41 @@
 
         @pl.when(me == 0)
         def _():
-            outbuf[chunk] = state.astype(BF16)
-            inbuf[chunk] = jnp.zeros(inbuf.shape[1:], BF16)
-            if seq_count > 1:
-                onward(chunk).start()
+            for part in range(LANES // HOP):
+                hop = chunk * (LANES // HOP) + part
+                outbuf[hop] = state[:, hop_lanes(part)].astype(BF16)
+                inbuf[hop] = jnp.zeros(inbuf.shape[1:], BF16)
+                if seq_count > 1:
+                    onward(hop).start()
+
+    def relay(hop):
+        if seq_count == 1 or hop >= hops:
+            return
+        chunk, part = hop * HOP // LANES, hop % (LANES // HOP)
+
+        @pl.when((me > 0) & (me < seq_count - 1))
+        def _():
+            onward(hop).wait_recv()
+            expand = expander(chunk)[:, hop_lanes(part)]
+            through = spread(grown[0], expand)
+            for s in range(1, spans):
+                through = through * spread(grown[s], expand)
+            outbuf[hop] = (
+                through * inbuf[hop].astype(F32) + total[:, hop_lanes(hop)]
+            ).astype(BF16)
+            onward(hop).start()
+
+    arriving = []
+    for k, (source, landing) in enumerate(
+        ((dx_ref, rx), (db_ref, rb), (dc_ref, rc), (ddt_ref, rdt))
+    ):
+        arriving += exchange(source.at[0], landing, send_in.at[k], recv_in.at[k])
+        mine_copy = pltpu.make_async_copy(source.at[0, me], landing.at[me], own_sem.at[k])
+        mine_copy.start()
+        arriving.append(mine_copy)
+
+    for hop in range(LANES // HOP):
+        relay(hop)
 
     for copy in arriving:
         copy.wait()
@@ -240,34 +275,14 @@
         extra = dec_scores[s][g] * jnp.exp(gap) * size
         return jnp.concatenate([main.astype(BF16), extra.astype(BF16)], axis=0)
 
+    ends = [chunks // 2, chunks - 1, chunks]
+    leaving = []
     for chunk in range(chunks):
         g = chunk * heads_chunk // per_group
         cols = slice(g * N, (g + 1) * N)
         expand = expander(chunk)
         grow = [spread(grown[s], expand) for s in range(spans)]
-        if seq_count > 1:
-
-            @pl.when(me > 0)
-            def _():
-                onward(chunk).wait_recv()
-
-            @pl.when((me > 0) & (me < seq_count - 1))
-            def _():
-                through = grow[0]
-                for s in range(1, spans):
-                    through = through * grow[s]
-                outbuf[chunk] = (
-                    through * inbuf[chunk].astype(F32) + total[:, lanes(chunk)]
-                ).astype(BF16)
-                onward(chunk).start()
-
-        incoming = inbuf[chunk]
-        outer = spread(outer_parts, expand)
-        skip = spread(skip_parts, expand)
-        from_block = None
-        from_carried = None
-        reach = incoming.astype(F32)
-        passed = None
+        inners = []
         for s in range(spans):
             at = slice(s * SPAN, (s + 1) * SPAN)
             inner = []
@@ -278,7 +293,27 @@
                 both = jnp.concatenate([x_pair * low, x_pair * high], axis=0)
                 left = jnp.concatenate([weights(head, s), weights(head + 1, s)], axis=1)
                 inner.append(dot(left, both))
-            inner = jnp.concatenate(inner, axis=1)
+            inners.append(jnp.concatenate(inner, axis=1))
+        hop = chunk * (LANES // HOP)
+        for part in range(LANES // HOP // 2):
+            relay(hop + LANES // HOP + part)
+        if seq_count > 1:
+
+            @pl.when(me == seq_count - 1)
+            def _():
+                for part in range(LANES // HOP):
+                    onward(hop + part).wait_recv()
+
+        incoming = jnp.concatenate([inbuf[hop + part] for part in range(LANES // HOP)], axis=1)
+        outer = spread(outer_parts, expand)
+        skip = spread(skip_parts, expand)
+        from_block = None
+        from_carried = None
+        reach = incoming.astype(F32)
+        passed = None
+        for s in range(spans):
+            at = slice(s * SPAN, (s + 1) * SPAN)
+            inner = inners[s]
             if s == 0:
                 held = incoming
             else:
@@ -301,21 +336,31 @@
         for k in range(STEPS):
             value = value + spread(fresh_parts[k], expand) * dot(fresh_pick[k], xd_part)
         res[:, lanes(chunk)] = jnp.where(present, value, 0.0)
-
-    for q in range(seq_count):
-        dres[q] = res[pl.ds(q * STEPS, STEPS), :].astype(BF16)
-    leaving = exchange(dres, rres, send_out, recv_out)
-    mine_copy = pltpu.make_async_copy(dres.at[me], rres.at[me], own_sem.at[0])
-    mine_copy.start()
-    for copy in leaving + [mine_copy]:
-        copy.wait()
-    dout_ref[0] = rres[...]
+        for part in range(LANES // HOP // 2, LANES // HOP):
+            relay(hop + LANES // HOP + part)
+        if chunk + 1 in ends:
+            piece = ends.index(chunk + 1)
+            begin = ends[piece - 1] if piece else 0
+            area = slice(begin * LANES, (chunk + 1) * LANES)
+            for q in range(seq_count):
+                dres[piece, q, :, : area.stop - area.start] = res[
+                    pl.ds(q * STEPS, STEPS), area
+                ].astype(BF16)
+            leaving.append((area, exchange(
+                dres.at[piece], rres.at[piece], send_out.at[piece], recv_out.at[piece]
+            )))
+
+    for piece, (area, copies) in enumerate(leaving):
+        for copy in copies:
+            copy.wait()
+        rres[piece, me] = dres[piece, me]
+        dout_ref[0, :, :, area] = rres[piece, :, :, : area.stop - area.start]
     if seq_count > 1:
 
         @pl.when(me < seq_count - 1)
         def _():
-            for chunk in range(chunks):
-                onward(chunk).wait_send()
+            for hop in range(hops):
+                onward(hop).wait_send()
 
 
 def shards(
@@ -326,7 +371,8 @@
     heads = dt_raw.shape[1]
     gn = bmat.shape[1]
     spans = tokens // SPAN
-    chunks = width // LANES
+    hops = width // HOP
+    half = width // 2
     rows = seq_count * STEPS
     vmem = pl.BlockSpec(memory_space=pltpu.VMEM)
     dma = pltpu.SemaphoreType.DMA
@@ -337,9 +383,12 @@
             jax.ShapeDtypeStruct((tokens, width), BF16),
             jax.ShapeDtypeStruct((1,) + slots + (width,), BF16),
         ),
-        in_specs=[vmem] * 12,
+        in_specs=[pl.BlockSpec(memory_space=pltpu.HBM)] * 3 + [vmem] * 9,
         out_specs=(vmem, vmem),
         scratch_shapes=[
+            pltpu.VMEM((tokens, width), BF16),
+            pltpu.VMEM((tokens, gn), BF16),
+            pltpu.VMEM((tokens, gn), BF16),
             pltpu.VMEM(slots + (width,), BF16),
             pltpu.VMEM(slots + (gn,), BF16),
             pltpu.VMEM(slots + (gn,), BF16),
@@ -349,25 +398,26 @@
             pltpu.VMEM((rows, gn), F32),
             pltpu.VMEM((rows, heads), F32),
             pltpu.VMEM((rows, width), F32),
-            pltpu.VMEM(slots + (width,), BF16),
-            pltpu.VMEM(slots + (width,), BF16),
-            pltpu.VMEM((chunks, N, LANES), BF16),
-            pltpu.VMEM((chunks, N, LANES), BF16),
+            pltpu.VMEM((3,) + slots + (half,), BF16),
+            pltpu.VMEM((3,) + slots + (half,), BF16),
+            pltpu.VMEM((hops, N, HOP), BF16),
+            pltpu.VMEM((hops, N, HOP), BF16),
             pltpu.VMEM((max(spans - 1, 1), N, width), F32),
             pltpu.VMEM((N, width), F32),
+            dma((3,)),
             dma((4, seq_count)),
             dma((4, seq_count)),
             dma((4,)),
-            dma((chunks,)),
-            dma((chunks,)),
-            dma((seq_count,)),
-            dma((seq_count,)),
+            dma((hops,)),
+            dma((hops,)),
+            dma((3, seq_count)),
+            dma((3, seq_count)),
         ],
         compiler_params=pltpu.CompilerParams(
             collective_id=0, has_side_effects=True, vmem_limit_bytes=40 * 1024 * 1024
         ),
     )(
-        ssm_input, bmat, cmat, dt_raw, a_log[None, :], d_skip[None, :],
+        ssm_input, bmat, cmat, dt_raw.T, a_log[None, :], d_skip[None, :],
         prompt_len[None, :], owner[None, :], dec_x, dec_b, dec_c, dec_dt,
     )
 

time: 38.7 us -> 51.9 us (1.34)
  Pallas kernels: 32.2 us -> 41.2 us
  local copies, waits for them, and re-layouts: 5.56 us -> 9.56 us
    pallas_call x1, Pallas kernels: 32.2 us -> 41.2 us  [shards(): pl.pallas_call(functools.partial(kernel, seq_count), out_shape=(jax.Shape...]
    unnamed x25 -> x26, local copies, waits for them, and re-layouts: 5.56 us -> 9.56 us
where the time goes in v2:
time: 51.9 us; the launch traced here: 51.4 us
  Pallas kernels  41.2 us (79%)
  local copies, waits for them, and re-layouts  9.56 us (18%)
  between operations  0.68 us (1%)
    pallas_call x1, Pallas kernels, shards(): pl.pallas_call(functools.partial(kernel, seq_count), out_shape=(jax.Shape...  41.2 us
    unnamed x26, local copies, waits for them, and re-layouts  9.56 us

profile of v2, /device:TPU:0, one launch (start us, length us, event | category | flops | bytes accessed | tf_op | source)
XLA Modules:
  0.0 51.4 jit_solution(17529900802175384994)
XLA Ops:
  0.6 0.0 copy-start.5
  0.6 0.0 copy-start.8
  0.7 0.0 copy-start.9
  0.7 0.7 %copy-done.5 = bf16[1,4,4,256]{3,2,1,0:T(4,128)(2,1)S(1)} copy-done((bf16[1,4,4,256]{3,2,1,0:T(4,128)(2,1)S(1)}, bf16[1,4,4,256]{3,2,1,0:T(4,128)(2,1)}, u32[]{:S(2)}) %copy-start.5) | copy-done | bytes 8216
  1.3 0.0 copy-done.8
  1.3 0.0 copy-done.9
  1.3 0.0 copy-start
  1.3 1.2 %copy-done = bf16[256,2048]{1,0:T(8,128)(2,1)S(1)} copy-done((bf16[256,2048]{1,0:T(8,128)(2,1)S(1)}, bf16[256,2048]{1,0:T(8,128)(2,1)}, u32[]{:S(2)}) %copy-start) | copy-done | bytes 1048600
  2.6 0.0 copy-start.1
  2.6 0.9 %copy-done.1 = bf16[256,256]{1,0:T(8,128)(2,1)S(1)} copy-done((bf16[256,256]{1,0:T(8,128)(2,1)S(1)}, bf16[256,256]{1,0:T(8,128)(2,1)}, u32[]{:S(2)}) %copy-start.1) | copy-done | bytes 131096
  3.5 0.0 copy-start.2
  3.5 0.9 %copy-done.2 = bf16[256,256]{1,0:T(8,128)(2,1)S(1)} copy-done((bf16[256,256]{1,0:T(8,128)(2,1)S(1)}, bf16[256,256]{1,0:T(8,128)(2,1)}, u32[]{:S(2)}) %copy-start.2) | copy-done | bytes 131096
  4.4 0.0 copy-start.3
  4.4 0.8 %copy-done.3 = bf16[1,4,4,2048]{3,2,1,0:T(4,128)(2,1)S(1)} copy-done((bf16[1,4,4,2048]{3,2,1,0:T(4,128)(2,1)S(1)}, bf16[1,4,4,2048]{3,2,1,0:T(4,128)(2,1)}, u32[]{:S(2)}) %copy-start.3) | copy-done | bytes 65560
  5.2 0.0 copy-start.4
  5.2 0.7 %copy-done.4 = bf16[256,32]{0,1:T(8,128)(2,1)S(1)} copy-done((bf16[256,32]{0,1:T(8,128)(2,1)S(1)}, bf16[256,32]{0,1:T(8,128)(2,1)}, u32[]{:S(2)}) %copy-start.4) | copy-done | bytes 16408
  5.9 0.0 copy-start.6
  5.9 0.7 %copy-done.6 = bf16[1,4,4,256]{3,2,1,0:T(4,128)(2,1)S(1)} copy-done((bf16[1,4,4,256]{3,2,1,0:T(4,128)(2,1)S(1)}, bf16[1,4,4,256]{3,2,1,0:T(4,128)(2,1)}, u32[]{:S(2)}) %copy-start.6) | copy-done | bytes 8216
  6.6 0.0 copy-start.7
  6.6 0.7 %copy-done.7 = bf16[1,4,4,32]{3,2,1,0:T(4,128)(2,1)S(1)} copy-done((bf16[1,4,4,32]{3,2,1,0:T(4,128)(2,1)S(1)}, bf16[1,4,4,32]{3,2,1,0:T(4,128)(2,1)}, u32[]{:S(2)}) %copy-start.7) | copy-done | bytes 1048
  7.3 0.0 copy-start.10
  7.3 0.7 %copy-done.10 = s32[8]{0:T(128)S(1)} copy-done((s32[8]{0:T(128)S(1)}, s32[8]{0:T(128)}, u32[]{:S(2)}) %copy-start.10) | copy-done | bytes 56
  8.0 0.0 copy-start.11
  8.0 0.7 %copy-done.11 = s32[8]{0:T(128)S(1)} copy-done((s32[8]{0:T(128)S(1)}, s32[8]{0:T(128)}, u32[]{:S(2)}) %copy-start.11) | copy-done | bytes 56
  8.6 41.2 %shard_map.131 = (bf16[256,2048]{1,0:T(8,128)(2,1)S(1)}, bf16[1,4,4,2048]{3,2,1,0:T(4,128)(2,1)S(1)}) custom-call(bf16[256,2048]{1,0:T(8,128)(2,1)S(1)} %copy-done, bf16[256,256]{1,0:T(8,128)(2,1)S(1)} %copy-done.1, bf16[256,256]{1,0:T(8,128)(2,1)S(1)} %copy-done.2, bf16[32,256]{1,0:T(8,128)(2,1)S(1)} %bitcast.5, f32[1,32]{1,0:T(1,128)S(1)} %bitcast.6, ...), custom_call_target="tpu_custom_call" | custom-call | tf_op jit(solution)/shard_map/pallas_call | solution.py:380
  49.8 1.0 %copy.16 = bf16[256,2048]{1,0:T(8,128)(2,1)} copy(bf16[256,2048]{1,0:T(8,128)(2,1)S(1)} %get-tuple-element.4) | data formatting | bytes 2097152
  50.8 0.6 %copy.17 = bf16[1,4,4,2048]{3,2,1,0:T(4,128)(2,1)} copy(bf16[1,4,4,2048]{3,2,1,0:T(4,128)(2,1)S(1)} %get-tuple-element.5) | data formatting | bytes 131072
Async XLA Ops:
  0.6 0.7 %copy-start.5 = (bf16[1,4,4,256]{3,2,1,0:T(4,128)(2,1)S(1)}, bf16[1,4,4,256]{3,2,1,0:T(4,128)(2,1)}, u32[]{:S(2)}) copy-start(bf16[1,4,4,256]{3,2,1,0:T(4,128)(2,1)} %db_ref.1) | copy-start | bytes 24580
  0.6 0.7 %copy-start.8 = (f32[32]{0:T(128)S(1)}, f32[32]{0:T(128)}, u32[]{:S(2)}) copy-start(f32[32]{0:T(128)} %param.16) | copy-start | bytes 388
  0.7 0.7 %copy-start.9 = (f32[32]{0:T(128)S(1)}, f32[32]{0:T(128)}, u32[]{:S(2)}) copy-start(f32[32]{0:T(128)} %param.17) | copy-start | bytes 388
  1.3 1.2 %copy-start = (bf16[256,2048]{1,0:T(8,128)(2,1)S(1)}, bf16[256,2048]{1,0:T(8,128)(2,1)}, u32[]{:S(2)}) copy-start(bf16[256,2048]{1,0:T(8,128)(2,1)} %x_hbm.1) | copy-start | bytes 3145732
  2.6 0.9 %copy-start.1 = (bf16[256,256]{1,0:T(8,128)(2,1)S(1)}, bf16[256,256]{1,0:T(8,128)(2,1)}, u32[]{:S(2)}) copy-start(bf16[256,256]{1,0:T(8,128)(2,1)} %b_hbm.1) | copy-start | bytes 393220
  3.5 0.9 %copy-start.2 = (bf16[256,256]{1,0:T(8,128)(2,1)S(1)}, bf16[256,256]{1,0:T(8,128)(2,1)}, u32[]{:S(2)}) copy-start(bf16[256,256]{1,0:T(8,128)(2,1)} %c_hbm.1) | copy-start | bytes 393220
  4.4 0.8 %copy-start.3 = (bf16[1,4,4,2048]{3,2,1,0:T(4,128)(2,1)S(1)}, bf16[1,4,4,2048]{3,2,1,0:T(4,128)(2,1)}, u32[]{:S(2)}) copy-start(bf16[1,4,4,2048]{3,2,1,0:T(4,128)(2,1)} %dx_ref.1) | copy-start | bytes 196612
  5.2 0.7 %copy-start.4 = (bf16[256,32]{0,1:T(8,128)(2,1)S(1)}, bf16[256,32]{0,1:T(8,128)(2,1)}, u32[]{:S(2)}) copy-start(bf16[256,32]{0,1:T(8,128)(2,1)} %param.15) | copy-start | bytes 49156
  5.9 0.7 %copy-start.6 = (bf16[1,4,4,256]{3,2,1,0:T(4,128)(2,1)S(1)}, bf16[1,4,4,256]{3,2,1,0:T(4,128)(2,1)}, u32[]{:S(2)}) copy-start(bf16[1,4,4,256]{3,2,1,0:T(4,128)(2,1)} %dc_ref.1) | copy-start | bytes 24580
  6.6 0.7 %copy-start.7 = (bf16[1,4,4,32]{3,2,1,0:T(4,128)(2,1)S(1)}, bf16[1,4,4,32]{3,2,1,0:T(4,128)(2,1)}, u32[]{:S(2)}) copy-start(bf16[1,4,4,32]{3,2,1,0:T(4,128)(2,1)} %ddt_ref.1) | copy-start | bytes 3076
  7.3 0.7 %copy-start.10 = (s32[8]{0:T(128)S(1)}, s32[8]{0:T(128)}, u32[]{:S(2)}) copy-start(s32[8]{0:T(128)} %param.18) | copy-start | bytes 100
  8.0 0.7 %copy-start.11 = (s32[8]{0:T(128)S(1)}, s32[8]{0:T(128)}, u32[]{:S(2)}) copy-start(s32[8]{0:T(128)} %param.19) | copy-start | bytes 100

commit v3 on v2

--- a/solution.py
+++ b/solution.py
@@ -64,10 +64,10 @@
     seq_count,
     x_hbm, b_hbm, c_hbm, dt_ref, alog_ref, skip_ref, len_ref, own_ref,
     dx_ref, db_ref, dc_ref, ddt_ref,
-    out_ref, dout_ref,
-    x_ref, b_ref, c_ref, rx, rb, rc, rdt, xd, bd, cd, dtd, res, dres, rres,
+    out_hbm, dout_ref,
+    x_ref, b_ref, c_ref, out_ref, rx, rb, rc, rdt, xd, bd, cd, dtd, res, dres, rres,
     inbuf, outbuf, first, total,
-    load_sem, send_in, recv_in, own_sem, send_state, recv_state, send_out, recv_out,
+    load_sem, store_sem, send_in, recv_in, own_sem, send_state, recv_state, send_out, recv_out,
 ):
     me = lax.axis_index("seq")
     tokens, width = x_ref.shape
@@ -134,9 +134,17 @@
     def lanes(chunk):
         return slice(chunk * LANES, (chunk + 1) * LANES)
 
+    pl.semaphore_wait(barrier, seq_count - 1)
+    arriving = []
+    for k, (source, landing) in enumerate(
+        ((dx_ref, rx), (db_ref, rb), (dc_ref, rc), (ddt_ref, rdt))
+    ):
+        arriving += exchange(source.at[0], landing, send_in.at[k], recv_in.at[k])
+        mine_copy = pltpu.make_async_copy(source.at[0, me], landing.at[me], own_sem.at[k])
+        mine_copy.start()
+        arriving.append(mine_copy)
     for copy in loads:
         copy.wait()
-    pl.semaphore_wait(barrier, seq_count - 1)
     b_t = [
         [b_ref[s * SPAN:(s + 1) * SPAN, g * N:(g + 1) * N].T for g in range(groups)]
         for s in range(spans)
@@ -193,15 +201,6 @@
                 through * inbuf[hop].astype(F32) + total[:, hop_lanes(hop)]
             ).astype(BF16)
             onward(hop).start()
-
-    arriving = []
-    for k, (source, landing) in enumerate(
-        ((dx_ref, rx), (db_ref, rb), (dc_ref, rc), (ddt_ref, rdt))
-    ):
-        arriving += exchange(source.at[0], landing, send_in.at[k], recv_in.at[k])
-        mine_copy = pltpu.make_async_copy(source.at[0, me], landing.at[me], own_sem.at[k])
-        mine_copy.start()
-        arriving.append(mine_copy)
 
     for hop in range(LANES // HOP):
         relay(hop)
@@ -276,7 +275,7 @@
         return jnp.concatenate([main.astype(BF16), extra.astype(BF16)], axis=0)
 
     ends = [chunks // 2, chunks - 1, chunks]
-    leaving = []
+    leaving, stores = [], []
     for chunk in range(chunks):
         g = chunk * heads_chunk // per_group
         cols = slice(g * N, (g + 1) * N)
@@ -330,6 +329,11 @@
                 if s == 0
                 else jnp.where(spot_span == s, carried[SPAN:], from_carried)
             )
+        store = pltpu.make_async_copy(
+            out_ref.at[:, lanes(chunk)], out_hbm.at[:, lanes(chunk)], store_sem.at[chunk]
+        )
+        store.start()
+        stores.append(store)
         state_part = spread(spot_parts, expand) * from_carried + from_block
         xd_part = x_dec[:, lanes(chunk)]
         value = spread(running_parts, expand) * state_part + skip * xd_part.astype(F32)
@@ -361,6 +365,9 @@
         def _():
             for hop in range(hops):
                 onward(hop).wait_send()
+
+    for store in stores:
+        store.wait()
 
 
 def shards(
@@ -384,11 +391,12 @@
             jax.ShapeDtypeStruct((1,) + slots + (width,), BF16),
         ),
         in_specs=[pl.BlockSpec(memory_space=pltpu.HBM)] * 3 + [vmem] * 9,
-        out_specs=(vmem, vmem),
+        out_specs=(pl.BlockSpec(memory_space=pltpu.HBM), vmem),
         scratch_shapes=[
             pltpu.VMEM((tokens, width), BF16),
             pltpu.VMEM((tokens, gn), BF16),
             pltpu.VMEM((tokens, gn), BF16),
+            pltpu.VMEM((tokens, width), BF16),
             pltpu.VMEM(slots + (width,), BF16),
             pltpu.VMEM(slots + (gn,), BF16),
             pltpu.VMEM(slots + (gn,), BF16),
@@ -405,6 +413,7 @@
             pltpu.VMEM((max(spans - 1, 1), N, width), F32),
             pltpu.VMEM((N, width), F32),
             dma((3,)),
+            dma((width // LANES,)),
             dma((4, seq_count)),
             dma((4, seq_count)),
             dma((4,)),
@@ -414,7 +423,7 @@
             dma((3, seq_count)),
         ],
         compiler_params=pltpu.CompilerParams(
-            collective_id=0, has_side_effects=True, vmem_limit_bytes=40 * 1024 * 1024
+            collective_id=0, has_side_effects=True, vmem_limit_bytes=63 * 1024 * 1024
         ),
     )(
         ssm_input, bmat, cmat, dt_raw.T, a_log[None, :], d_skip[None, :],

time: 51.9 us -> 37.5 us (0.72)
  Pallas kernels: 41.2 us -> 33.6 us
  local copies, waits for them, and re-layouts: 9.56 us -> 2.97 us
    pallas_call x1, Pallas kernels: 41.2 us -> 33.6 us  [shards(): pl.pallas_call(functools.partial(kernel, seq_count), out_shape=(jax.Shape...]
    unnamed x26 -> x4, local copies, waits for them, and re-layouts: 9.56 us -> 2.97 us
where the time goes in v3:
time: 37.5 us; the launch traced here: 37.3 us
  Pallas kernels  33.6 us (90%)
  local copies, waits for them, and re-layouts  2.97 us (8%)
  between operations  0.65 us (2%)
    pallas_call x1, Pallas kernels, shards(): pl.pallas_call(functools.partial(kernel, seq_count), out_shape=(jax.Shape...  33.6 us
    unnamed x4, local copies, waits for them, and re-layouts  2.97 us

profile of v3, /device:TPU:0, one launch (start us, length us, event | category | flops | bytes accessed | tf_op | source)
XLA Modules:
  0.0 37.3 jit_solution(17378452260454636690)
XLA Ops:
  0.6 33.6 %shard_map.131 = (bf16[256,2048]{1,0:T(8,128)(2,1)}, bf16[1,4,4,2048]{3,2,1,0:T(4,128)(2,1)}) custom-call(bf16[256,2048]{1,0:T(8,128)(2,1)} %x_hbm.1, bf16[256,256]{1,0:T(8,128)(2,1)} %b_hbm.1, bf16[256,256]{1,0:T(8,128)(2,1)} %c_hbm.1, bf16[32,256]{1,0:T(8,128)(2,1)} %bitcast.5, f32[1,32]{1,0:T(1,128)} %bitcast.6, f32[1,32]{1,0:T(1,128)} %bitcast.7, ...), custom_call_target="tpu_custom_call" | custom-call | tf_op jit(solution)/shard_map/pallas_call | solution.py:387
  34.3 0.0 copy-start
  34.3 2.3 %copy.16 = bf16[256,2048]{1,0:T(8,128)(2,1)} copy(bf16[256,2048]{1,0:T(8,128)(2,1)} %get-tuple-element.4) | data formatting | bytes 2097152
  36.6 0.0 copy-done
  36.6 0.6 %copy.17 = bf16[1,4,4,2048]{3,2,1,0:T(4,128)(2,1)} copy(bf16[1,4,4,2048]{3,2,1,0:T(4,128)(2,1)S(1)} %copy-done) | data formatting | bytes 131072
Async XLA Ops:
  34.3 2.3 %copy-start = (bf16[1,4,4,2048]{3,2,1,0:T(4,128)(2,1)S(1)}, bf16[1,4,4,2048]{3,2,1,0:T(4,128)(2,1)}, u32[]{:S(2)}) copy-start(bf16[1,4,4,2048]{3,2,1,0:T(4,128)(2,1)} %get-tuple-element.5) | copy-start | bytes 196612

commit v4 on v3

--- a/solution.py
+++ b/solution.py
@@ -274,7 +274,7 @@
         extra = dec_scores[s][g] * jnp.exp(gap) * size
         return jnp.concatenate([main.astype(BF16), extra.astype(BF16)], axis=0)
 
-    ends = [chunks // 2, chunks - 1, chunks]
+    ends = [chunks]
     leaving, stores = [], []
     for chunk in range(chunks):
         g = chunk * heads_chunk // per_group
@@ -379,7 +379,7 @@
     gn = bmat.shape[1]
     spans = tokens // SPAN
     hops = width // HOP
-    half = width // 2
+    half = width
     rows = seq_count * STEPS
     vmem = pl.BlockSpec(memory_space=pltpu.VMEM)
     dma = pltpu.SemaphoreType.DMA

time: 37.5 us -> 36.8 us (0.981)
  Pallas kernels: 33.6 us -> 33 us
    pallas_call x1, Pallas kernels: 33.6 us -> 33 us  [shards(): pl.pallas_call(functools.partial(kernel, seq_count), out_shape=(jax.Shape...]
where the time goes in v4:
time: 36.8 us; the launch traced here: 36.7 us
  Pallas kernels  33 us (90%)
  local copies, waits for them, and re-layouts  2.97 us (8%)
  between operations  0.65 us (2%)
    pallas_call x1, Pallas kernels, shards(): pl.pallas_call(functools.partial(kernel, seq_count), out_shape=(jax.Shape...  33 us
    unnamed x4, local copies, waits for them, and re-layouts  2.97 us

profile of v4, /device:TPU:0, one launch (start us, length us, event | category | flops | bytes accessed | tf_op | source)
XLA Modules:
  0.0 36.7 jit_solution(11637556398770978791)
XLA Ops:
  0.6 33.0 %shard_map.131 = (bf16[256,2048]{1,0:T(8,128)(2,1)}, bf16[1,4,4,2048]{3,2,1,0:T(4,128)(2,1)}) custom-call(bf16[256,2048]{1,0:T(8,128)(2,1)} %x_hbm.1, bf16[256,256]{1,0:T(8,128)(2,1)} %b_hbm.1, bf16[256,256]{1,0:T(8,128)(2,1)} %c_hbm.1, bf16[32,256]{1,0:T(8,128)(2,1)} %bitcast.5, f32[1,32]{1,0:T(1,128)} %bitcast.6, f32[1,32]{1,0:T(1,128)} %bitcast.7, ...), custom_call_target="tpu_custom_call" | custom-call | tf_op jit(solution)/shard_map/pallas_call | solution.py:387
  33.7 0.0 copy-start
  33.7 2.3 %copy.16 = bf16[256,2048]{1,0:T(8,128)(2,1)} copy(bf16[256,2048]{1,0:T(8,128)(2,1)} %get-tuple-element.4) | data formatting | bytes 2097152
  36.0 0.0 copy-done
  36.0 0.6 %copy.17 = bf16[1,4,4,2048]{3,2,1,0:T(4,128)(2,1)} copy(bf16[1,4,4,2048]{3,2,1,0:T(4,128)(2,1)S(1)} %copy-done) | data formatting | bytes 131072
Async XLA Ops:
  33.7 2.3 %copy-start = (bf16[1,4,4,2048]{3,2,1,0:T(4,128)(2,1)S(1)}, bf16[1,4,4,2048]{3,2,1,0:T(4,128)(2,1)}, u32[]{:S(2)}) copy-start(bf16[1,4,4,2048]{3,2,1,0:T(4,128)(2,1)} %get-tuple-element.5) | copy-start | bytes 196612

commit v5 on v4

--- a/solution.py
+++ b/solution.py
@@ -294,7 +294,7 @@
                 inner.append(dot(left, both))
             inners.append(jnp.concatenate(inner, axis=1))
         hop = chunk * (LANES // HOP)
-        for part in range(LANES // HOP // 2):
+        for part in range(LANES // HOP):
             relay(hop + LANES // HOP + part)
         if seq_count > 1:
 
@@ -340,7 +340,7 @@
         for k in range(STEPS):
             value = value + spread(fresh_parts[k], expand) * dot(fresh_pick[k], xd_part)
         res[:, lanes(chunk)] = jnp.where(present, value, 0.0)
-        for part in range(LANES // HOP // 2, LANES // HOP):
+        for part in range(0):
             relay(hop + LANES // HOP + part)
         if chunk + 1 in ends:
             piece = ends.index(chunk + 1)

time: 36.8 us -> 36.7 us (level)
  no operation moved by 1% of the time
where the time goes in v5:
time: 36.7 us; the launch traced here: 36.5 us
  Pallas kernels  32.9 us (90%)
  local copies, waits for them, and re-layouts  2.97 us (8%)
  between operations  0.65 us (2%)
    pallas_call x1, Pallas kernels, shards(): pl.pallas_call(functools.partial(kernel, seq_count), out_shape=(jax.Shape...  32.9 us
    unnamed x4, local copies, waits for them, and re-layouts  2.97 us

profile of v5, /device:TPU:0, one launch (start us, length us, event | category | flops | bytes accessed | tf_op | source)
XLA Modules:
  0.0 36.5 jit_solution(7152341181616394464)
XLA Ops:
  0.6 32.9 %shard_map.131 = (bf16[256,2048]{1,0:T(8,128)(2,1)}, bf16[1,4,4,2048]{3,2,1,0:T(4,128)(2,1)}) custom-call(bf16[256,2048]{1,0:T(8,128)(2,1)} %x_hbm.1, bf16[256,256]{1,0:T(8,128)(2,1)} %b_hbm.1, bf16[256,256]{1,0:T(8,128)(2,1)} %c_hbm.1, bf16[32,256]{1,0:T(8,128)(2,1)} %bitcast.5, f32[1,32]{1,0:T(1,128)} %bitcast.6, f32[1,32]{1,0:T(1,128)} %bitcast.7, ...), custom_call_target="tpu_custom_call" | custom-call | tf_op jit(solution)/shard_map/pallas_call | solution.py:387
  33.5 0.0 copy-start
  33.5 2.3 %copy.16 = bf16[256,2048]{1,0:T(8,128)(2,1)} copy(bf16[256,2048]{1,0:T(8,128)(2,1)} %get-tuple-element.4) | data formatting | bytes 2097152
  35.9 0.0 copy-done
  35.9 0.6 %copy.17 = bf16[1,4,4,2048]{3,2,1,0:T(4,128)(2,1)} copy(bf16[1,4,4,2048]{3,2,1,0:T(4,128)(2,1)S(1)} %copy-done) | data formatting | bytes 131072
Async XLA Ops:
  33.5 2.3 %copy-start = (bf16[1,4,4,2048]{3,2,1,0:T(4,128)(2,1)S(1)}, bf16[1,4,4,2048]{3,2,1,0:T(4,128)(2,1)}, u32[]{:S(2)}) copy-start(bf16[1,4,4,2048]{3,2,1,0:T(4,128)(2,1)} %get-tuple-element.5) | copy-start | bytes 196612
